TPU v7x, 512 devices: a whole 4x4x16 slice. The times are simulated.
512 devices in a mesh: tile: 8 (over x, core), beam: 64 (over y, z).
Axes of the slice: x: 4, y: 4, z: 16, core: 2. Of those that a mesh axis runs over, the one named last changes fastest.
Arguments:
- echoes: bfloat16 [2, 2048, 32768], P(None, 'tile', 'beam'), may hold values from -160 to 160
- steer: bfloat16 [2, 2048, 2048], P(None, None, 'tile'), may hold values from -0.09375 to 0.09375
- code: bfloat16 [2, 8], replicated, may hold values from -1 to 1
- beam_order: int32 [2048], replicated, may hold values from 0 to 2047, each once
- dwell: int32 [2048], replicated, may hold values from 256 to 1024, as said below
- code_len: int32 [2048], replicated, may hold values from 1 to 8, as said below
Outputs:
- spectrum: float32 [2048, 2, 32, 1024], P(('tile', 'beam'))
Inputs may be any that keep to these rules, and one draw needn't show every extreme that they name: dwell[b] counts the leading pulses that beam b keeps; some beam keeps all 1024. `code_len`: some beam uses all 8 taps.
All inputs are finite; a program needn't handle non-finite values.
Results may differ from a plain program's by a relative error of at most 0.015.
Values may be sent and summed in bfloat16 or wider, within the bound.
A program may use at most 64 MiB of HBM per device.

v0:
```python
import math

import jax
import jax.numpy as jnp
from jax import lax
from jax.sharding import PartitionSpec as P

G = 32


def copy_for_each(x, axis):
    count = lax.axis_size(axis)
    return lax.all_to_all(jnp.broadcast_to(x[None], (count, *x.shape)), axis, 0, 0, tiled=True)


def taken_together(x, axis):
    everything = copy_for_each(x, axis)
    return jnp.sum(everything, axis=0)


def cut_along(x, dim, count):
    before, after = (x.shape[:dim], x.shape[dim + 1 :])
    return jnp.moveaxis(x.reshape(*before, count, -1, *after), dim, 0)


def sum_at_owner(x, axis, dim):
    pieces = cut_along(x, dim, lax.axis_size(axis))
    arrived = lax.all_to_all(pieces, axis, split_axis=0, concat_axis=0, tiled=True)
    return arrived.astype(jnp.float32).sum(axis=0)


def complex_block(weight_re, weight_im):
    upper = jnp.concatenate([weight_re, -weight_im], axis=1)
    lower = jnp.concatenate([weight_im, weight_re], axis=1)
    return jnp.stack([upper, lower], axis=1).reshape(2 * weight_re.shape[0], 2 * weight_re.shape[1])


def phase_table(rows, cols, period):
    row_index = jnp.arange(rows, dtype=jnp.int32)
    col_index = jnp.arange(cols, dtype=jnp.int32)
    phase = row_index[:, None] * col_index[None, :] % period
    angle = phase.astype(jnp.float32) * (2.0 * math.pi / period)
    return (jnp.cos(angle), -jnp.sin(angle))


def split_length(total):
    smaller = 1
    for candidate in range(1, math.isqrt(total) + 1):
        if total % candidate == 0:
            smaller = candidate
    return (smaller, total // smaller)


def compress(values, code, lens, limits, first_pulse):
    gates = values.shape[3]
    taps = code.shape[1]
    padded = jnp.pad(values, ((0, 0), (0, 0), (0, 0), (0, taps)))
    code_re = code[0].astype(jnp.float32)
    code_im = code[1].astype(jnp.float32)
    out_re = jnp.zeros((values.shape[0], values.shape[2], gates), jnp.float32)
    out_im = jnp.zeros((values.shape[0], values.shape[2], gates), jnp.float32)
    for tap in range(taps):
        live = (tap < lens).astype(jnp.float32)[:, None, None]
        shift_re = padded[:, 0, :, tap : tap + gates]
        shift_im = padded[:, 1, :, tap : tap + gates]
        out_re = out_re + live * (code_re[tap] * shift_re + code_im[tap] * shift_im)
        out_im = out_im + live * (code_re[tap] * shift_im - code_im[tap] * shift_re)
    pulse_index = first_pulse + jnp.arange(values.shape[2], dtype=jnp.int32)
    keep = (pulse_index[None, :] < limits[:, None]).astype(jnp.float32)[:, None, :, None]
    return (jnp.stack([out_re, out_im], axis=1) * keep).astype(jnp.bfloat16)


def highest(form, left, right):
    return jnp.einsum(form, left, right, precision=lax.Precision.HIGHEST)


def on_device(echoes, steer, code, beam_order, dwell, code_len):
    tiles = lax.axis_size("tile")
    owners = lax.axis_size("beam")
    chans = echoes.shape[1]
    columns = echoes.shape[2]
    beam_total = steer.shape[1]
    pulses_dev = columns // G
    pulses_all = pulses_dev * owners
    tile_beams = beam_total // tiles
    values = echoes.astype(jnp.float32)
    local_power = jnp.sum(values * values, axis=(0, 2))
    power = taken_together(local_power, "beam") / (pulses_all * G)
    gain = lax.rsqrt(power + 1e-05)
    ordered = jnp.take(steer, beam_order, axis=1)
    weights = (ordered.astype(jnp.float32) * gain).astype(jnp.bfloat16)
    stacked = complex_block(weights[0], weights[1])
    flat = echoes.reshape(2 * chans, columns)
    summed = sum_at_owner(
        jnp.dot(stacked, flat, preferred_element_type=jnp.float32)
        .reshape(tile_beams * lax.axis_size("tile"), 2, columns)
        .astype(jnp.bfloat16),
        "tile",
        0,
    )
    rounded = lax.optimization_barrier(summed.astype(jnp.bfloat16))
    beams = rounded.astype(jnp.float32).reshape(tile_beams, 2, pulses_dev, G)
    first_slot = lax.axis_index("tile") * tile_beams
    slot_ids = lax.dynamic_slice_in_dim(beam_order, first_slot, tile_beams, 0)
    lens = jnp.take(code_len, slot_ids)
    limits = jnp.take(dwell, slot_ids)
    compressed = compress(beams, code, lens, limits, lax.axis_index("beam") * pulses_dev)
    scale = 1.0 / math.sqrt(pulses_all)
    inner_len, outer_len = split_length(pulses_all)
    outer_re, outer_im = phase_table(outer_len, outer_len, outer_len)
    twist_re, twist_im = phase_table(inner_len, outer_len, pulses_all)
    inner_re, inner_im = phase_table(inner_len, inner_len, inner_len)
    block = lax.all_to_all(compressed, "beam", split_axis=0, concat_axis=2, tiled=True)
    count_beams = block.shape[0]
    gates = block.shape[3]
    wide = block.astype(jnp.float32)
    real_part = wide[:, 0].reshape(count_beams, outer_len, inner_len, gates)
    imag_part = wide[:, 1].reshape(count_beams, outer_len, inner_len, gates)
    section_re = highest("nbag,bk->nakg", real_part, outer_re) - highest(
        "nbag,bk->nakg", imag_part, outer_im
    )
    section_im = highest("nbag,bk->nakg", imag_part, outer_re) + highest(
        "nbag,bk->nakg", real_part, outer_im
    )
    turned_re = section_re * twist_re[None, :, :, None] - section_im * twist_im[None, :, :, None]
    turned_im = section_re * twist_im[None, :, :, None] + section_im * twist_re[None, :, :, None]
    final_re = highest("nakg,aq->ngqk", turned_re, inner_re) - highest(
        "nakg,aq->ngqk", turned_im, inner_im
    )
    final_im = highest("nakg,aq->ngqk", turned_im, inner_re) + highest(
        "nakg,aq->ngqk", turned_re, inner_im
    )
    joined = jnp.stack([final_re, final_im], axis=1).reshape(count_beams, 2, gates, pulses_all)
    return joined * scale


def solution(mesh):
    placed = (P(None, "tile", "beam"), P(None, None, "tile"), P(), P(), P(), P())
    return jax.shard_map(
        on_device,
        mesh=mesh,
        in_specs=placed,
        out_specs=P(("tile", "beam"), None, None, None),
        check_vma=False,
    )
```

profile of v0, /device:TPU:24, one launch (start us, length us, event | category | flops | bytes accessed | tf_op | source)
XLA Modules:
  0.0 227.7 jit_solution(12904511989247915631)
XLA Ops:
  2.0 18.7 %all-to-all-start = ((f32[64,1,256]{2,1,0:T(1,128)}), f32[64,1,256]{2,1,0:T(1,128)S(1)}, u32[]{:S(2)}, u32[]{:S(2)}) async-start(f32[64,1,256]{2,1,0:T(1,128)} %broadcast_in_dim.23), calls=%async_computation | async-start | bytes 131072 | tf_op jit(solution)/shard_map/all_to_all | solution.py:13
  21.5 20.0 %gather_fusion = bf16[2048,2,256]{2,0,1:T(8,128)(2,1)} fusion(bf16[2,2048,256]{2,1,0:T(8,128)(2,1)S(1)} %copy-done, s32[2048]{0:T(1024)S(1)} %fusion.58), kind=kCustom, calls=%fused_computation.2 | custom fusion | bytes 4202496 | tf_op jit(solution)/shard_map/jit(_take)/gather | solution.py:90
  41.6 1.9 fusion.7
  44.8 2.3 %fusion.4 = bf16[2048,2,512]{2,0,1:T(8,128)(2,1)S(1)} fusion(bf16[512,512,1]{1,0,2:T(8,128)(2,1)S(1)} %bitcast.95, bf16[2048,1,512]{2,0,1:T(8,128)(2,1)S(1)} %get-tuple-element.15, bf16[2048,1,512]{2,0,1:T(8,128)(2,1)S(1)} %get-tuple-element.14), kind=kOutput, calls=%fused_computation.8 | convolution fusion | flops 2151677952 | bytes 8912896 | tf_op jit(solution)/shard_map/dot_general | solution.py:95
  47.2 2.4 %copy.87 = bf16[8,256,2,512]{3,1,2,0:T(8,128)(2,1)} copy(bf16[8,256,2,512]{3,1,0,2:T(8,128)(2,1)S(1)} %bitcast.94) | data formatting | bytes 8388608 | tf_op jit(solution)/shard_map/reshape | solution.py:23
  49.6 4.9 %all-to-all-start.1 = ((bf16[8,256,2,512]{3,1,2,0:T(8,128)(2,1)}), bf16[8,256,2,512]{3,1,2,0:T(8,128)(2,1)}, u32[]{:S(2)}, u32[]{:S(2)}) async-start(bf16[8,256,2,512]{3,1,2,0:T(8,128)(2,1)} %copy.87), calls=%async_computation.1 | async-start | bytes 8388608 | tf_op jit(solution)/shard_map/all_to_all | solution.py:28
  59.0 44.9 %all-to-all-done.1 = bf16[8,256,2,512]{3,1,2,0:T(8,128)(2,1)} async-done(((bf16[8,256,2,512]{3,1,2,0:T(8,128)(2,1)}), bf16[8,256,2,512]{3,1,2,0:T(8,128)(2,1)}, u32[]{:S(2)}, u32[]{:S(2)}) %all-to-all-start.1) | async-done | bytes 4194336 | tf_op jit(solution)/shard_map/all_to_all | solution.py:28
  103.9 3.7 %reduce_sum.32 = bf16[256,2,512]{2,0,1:T(8,128)(2,1)} reduce(bf16[8,256,2,512]{3,1,2,0:T(8,128)(2,1)} %all-to-all-done.1, bf16[]{:T(256)} %constant.86.clone.1), dimensions={0}, to_apply=%region_2.0 | reduce | flops 1835008 | bytes 4718594 | tf_op jit(solution)/shard_map/reduce_sum | solution.py:29
  108.9 11.0 %multiply_add_fusion = f32[256,1,16,32]{0,3,2,1:T(8,128)S(1)} fusion(f32[256,2,16,32]{0,3,2,1:T(8,128)S(1)} %bitcast.86, f32[]{:T(128)} %bitcast.27, f32[]{:T(128)} %bitcast.26, f32[256]{0:T(256)S(1)} %get-tuple-element.22, f32[]{:T(128)} %bitcast.25, f32[]{:T(128)} %bitcast.24, f32[256]{0:T(256)S(1)} %get-tuple-element.17, f32[]{:T(128)} %bitcast.23, ...), kind=kLoop, calls=%fused_computation.56 | loop fusion | flops 5111808 | bytes 2629696 | tf_op jit(solution)/shard_map/add | solution.py:67
  119.9 11.0 %multiply_add_fusion.1 = f32[256,1,16,32]{0,3,2,1:T(8,128)S(1)} fusion(f32[256,2,16,32]{0,3,2,1:T(8,128)S(1)} %bitcast.87, f32[]{:T(128)} %bitcast.27, f32[]{:T(128)} %bitcast.26, f32[256]{0:T(256)S(1)} %get-tuple-element.22, f32[]{:T(128)} %bitcast.25, f32[]{:T(128)} %bitcast.24, f32[256]{0:T(256)S(1)} %get-tuple-element.17, f32[]{:T(128)} %bitcast.23, ...), kind=kLoop, calls=%fused_computation.57 | loop fusion | flops 5111808 | bytes 2629696 | tf_op jit(solution)/shard_map/add | solution.py:66
  131.0 3.7 %copy.90 = bf16[256,2,16,32]{3,2,1,0:T(8,128)(2,1)} copy(bf16[256,2,16,32]{0,3,2,1:T(8,128)(2,1)S(1)} %fusion.22) | data formatting | bytes 1048576 | tf_op jit(solution)/shard_map/convert_element_type | solution.py:70
  134.7 4.5 %reshape.194 = bf16[64,2,2048]{2,1,0:T(2,128)(2,1)} reshape(bf16[256,2,16,32]{3,2,1,0:T(8,128)(2,1)} %copy.90) | data formatting | bytes 1048576
  139.2 15.1 %all-to-all-start.2 = ((bf16[64,2,2048]{2,1,0:T(2,128)(2,1)}), bf16[64,2,2048]{2,1,0:T(2,128)(2,1)S(1)}, u32[]{:S(2)}, u32[]{:S(2)}) async-start(bf16[64,2,2048]{2,1,0:T(2,128)(2,1)} %reshape.194), calls=%async_computation.2 | async-start | bytes 1048576 | tf_op jit(solution)/shard_map/all_to_all | solution.py:113
  154.6 30.9 %all-to-all-done.2 = bf16[64,2,2048]{2,1,0:T(2,128)(2,1)S(1)} async-done(((bf16[64,2,2048]{2,1,0:T(2,128)(2,1)}), bf16[64,2,2048]{2,1,0:T(2,128)(2,1)S(1)}, u32[]{:S(2)}, u32[]{:S(2)}) %all-to-all-start.2) | async-done | bytes 524320 | tf_op jit(solution)/shard_map/all_to_all | solution.py:113
  185.5 2.0 reshape.195
  187.6 2.0 copy.91
  194.9 3.0 %fusion.10 = f32[32,4,32,32]{3,0,2,1:T(8,128)S(1)} fusion(f32[4,32,32,32]{3,2,1,0:T(8,128)S(1)} %get-tuple-element.9), kind=kOutput, calls=%fused_computation.34 | convolution fusion | flops 50345984 | bytes 1048576 | tf_op jit(solution)/shard_map/nakg,aq->ngqk/dot_general | solution.py:74
  198.0 4.3 %fusion.12 = f32[32,4,32,32]{3,0,2,1:T(8,128)} fusion(f32[4,32,32,32]{3,2,1,0:T(8,128)S(1)} %get-tuple-element.9), kind=kOutput, calls=%fused_computation.36 | convolution fusion | flops 50347008 | bytes 1048576 | tf_op jit(solution)/shard_map/nakg,aq->ngqk/dot_general | solution.py:74
  202.3 4.7 %add_bitcast_fusion = f32[4,32,32,32]{1,2,3,0:T(8,128)} fusion(f32[32,4,32,32]{3,0,2,1:T(8,128)S(1)} %fusion.10, f32[4,32,32,32]{3,2,1,0:T(8,128)S(1)} %get-tuple-element.8), kind=kOutput, calls=%fused_computation.18 | convolution fusion | flops 50478080 | bytes 1572864 | tf_op jit(solution)/shard_map/nakg,aq->ngqk/dot_general | solution.py:74
  207.0 4.1 %copy.105 = f32[4,32,32,32]{3,2,1,0:T(8,128)} copy(f32[4,32,32,32]{1,2,3,0:T(8,128)} %add_bitcast_fusion) | data formatting | bytes 1048576 | tf_op jit(solution)/shard_map/add | solution.py:130
  211.1 2.4 %stack.28 = f32[4,1,32,1024]{3,2,0,1:T(8,128)S(1)} reshape(f32[4,32,32,32]{3,2,1,0:T(8,128)} %copy.105) | data formatting | bytes 1048576 | tf_op jit(solution)/shard_map/stack | solution.py:133
  213.5 6.5 %subtract_bitcast_fusion = f32[4,32,32,32]{1,2,3,0:T(8,128)} fusion(f32[32,4,32,32]{3,0,2,1:T(8,128)} %fusion.12, f32[4,32,32,32]{3,2,1,0:T(8,128)} %copy-done.3), kind=kOutput, calls=%fused_computation.19 | convolution fusion | flops 50477056 | bytes 1572864 | tf_op jit(solution)/shard_map/nakg,aq->ngqk/dot_general | solution.py:74
  220.0 4.1 %copy.102 = f32[4,32,32,32]{3,2,1,0:T(8,128)} copy(f32[4,32,32,32]{1,2,3,0:T(8,128)} %subtract_bitcast_fusion) | data formatting | bytes 1048576 | tf_op jit(solution)/shard_map/sub | solution.py:127
  224.1 2.4 %stack.27 = f32[4,1,32,1024]{3,2,0,1:T(8,128)S(1)} reshape(f32[4,32,32,32]{3,2,1,0:T(8,128)} %copy.102) | data formatting | bytes 1048576 | tf_op jit(solution)/shard_map/stack | solution.py:133
  (48 shorter events, 16.8 us)
Async XLA Ops:
  0.0 21.5 %copy-start = (bf16[2,2048,256]{2,1,0:T(8,128)(2,1)S(1)}, bf16[2,2048,256]{2,1,0:T(8,128)(2,1)}, u32[]{:S(2)}) copy-start(bf16[2,2048,256]{2,1,0:T(8,128)(2,1)} %param.9) | copy-start | bytes 6291460
  2.0 39.5 %all-to-all-start = ((f32[64,1,256]{2,1,0:T(1,128)}), f32[64,1,256]{2,1,0:T(1,128)S(1)}, u32[]{:S(2)}, u32[]{:S(2)}) async-start(f32[64,1,256]{2,1,0:T(1,128)} %broadcast_in_dim.23), calls=%async_computation | async-start | bytes 131072 | tf_op jit(solution)/shard_map/all_to_all | solution.py:13
  21.5 20.0 %copy-start.5 = (s32[2048]{0:T(1024)S(1)}, s32[2048]{0:T(1024)}, u32[]{:S(2)}) copy-start(s32[2048]{0:T(1024)} %param.11) | copy-start | bytes 24580
  43.8 1.0 copy-start.4
  49.6 5.0 %copy-start.1 = (s32[2048]{0:T(1024)S(1)}, s32[2048]{0:T(1024)}, u32[]{:S(2)}) copy-start(s32[2048]{0:T(1024)} %param.13) | copy-start | bytes 24580
  49.6 6.7 %copy-start.2 = (s32[2048]{0:T(1024)S(1)}, s32[2048]{0:T(1024)}, u32[]{:S(2)}) copy-start(s32[2048]{0:T(1024)} %param.12) | copy-start | bytes 24580
  49.6 54.3 %all-to-all-start.1 = ((bf16[8,256,2,512]{3,1,2,0:T(8,128)(2,1)}), bf16[8,256,2,512]{3,1,2,0:T(8,128)(2,1)}, u32[]{:S(2)}, u32[]{:S(2)}) async-start(bf16[8,256,2,512]{3,1,2,0:T(8,128)(2,1)} %copy.87), calls=%async_computation.1 | async-start | bytes 8388608 | tf_op jit(solution)/shard_map/all_to_all | solution.py:28
  54.5 3.6 %copy-start.6 = (bf16[2,8]{1,0:T(2,128)(2,1)S(1)}, bf16[2,8]{1,0:T(2,128)(2,1)}, u32[]{:S(2)}) copy-start(bf16[2,8]{1,0:T(2,128)(2,1)} %param.10) | copy-start | bytes 100
  139.2 46.4 %all-to-all-start.2 = ((bf16[64,2,2048]{2,1,0:T(2,128)(2,1)}), bf16[64,2,2048]{2,1,0:T(2,128)(2,1)S(1)}, u32[]{:S(2)}, u32[]{:S(2)}) async-start(bf16[64,2,2048]{2,1,0:T(2,128)(2,1)} %reshape.194), calls=%async_computation.2 | async-start | bytes 1048576 | tf_op jit(solution)/shard_map/all_to_all | solution.py:113
  194.9 7.4 %copy-start.3 = (f32[4,32,32,32]{3,2,1,0:T(8,128)}, f32[4,32,32,32]{3,2,1,0:T(8,128)S(1)}, u32[]{:S(2)}) copy-start(f32[4,32,32,32]{3,2,1,0:T(8,128)S(1)} %get-tuple-element.8) | copy-start | bytes 1572868
where the time goes:
time: 229 us; the launch traced here: 228 us
  waiting for transfers between devices  75.8 us (33%)
  local copies, waits for them, and re-layouts  55.9 us (24%)
  starting transfers between devices  38.7 us (17%)
  other arithmetic  30.9 us (13%)
  matrix products  26.1 us (11%)
    all_to_all x1, waiting for transfers between devices, sum_at_owner(): lax.all_to_all(pieces, axis, split_axis=0, concat_axis=0, tiled=True)  44.9 us
    all_to_all x1, waiting for transfers between devices, on_device(): lax.all_to_all(compressed, 'beam', split_axis=0, concat_axis=2, tiled=True)  30.9 us
    dot_general x8, matrix products, highest(): return jnp.einsum(form, left, right, precision=lax.Precision.HIGHEST)  23.8 us
    gather x1, local copies, waits for them, and re-layouts, on_device(): ordered = jnp.take(steer, beam_order, axis=1)  20 us
    all_to_all x1, starting transfers between devices, copy_for_each(): lax.all_to_all(jnp.broadcast_to(x[None], (count, *x.shape)), axis, 0, 0,...  18.7 us
    all_to_all x1, starting transfers between devices, on_device(): lax.all_to_all(compressed, 'beam', split_axis=0, concat_axis=2, tiled=True)  15.1 us
    add x1, other arithmetic, compress(): out_im = out_im + live * (code_re[tap] * shift_im - code_im[tap] * shift_re)  11 us
    add x1, other arithmetic, compress(): out_re = out_re + live * (code_re[tap] * shift_re + code_im[tap] * shift_im)  11 us
  transfers between devices with their start and end apart: 3, of which 2 were waited for; matrix products, arithmetic and copies ran while one was open for 11% of the time, Pallas kernels for 0%

commit v1 on v0

v1 whole, which is shorter than its diff:
```python
import math

import jax
import jax.numpy as jnp
import numpy as np
from jax import lax
from jax.experimental import pallas as pl
from jax.experimental.pallas import tpu as pltpu
from jax.sharding import PartitionSpec as P

G = 32
TAPS = 8
LANES = 128
MESH = pl.DeviceIdType.MESH
F32 = jnp.float32
BF16 = jnp.bfloat16


def exchange_kernel(
    nb,
    echo_hbm, steer_hbm, order_ref, dwell_ref, lens_ref, code_ref,
    out_ref,
    echo, steer, cols, perm, perm_out, power, gains, limit, pulses, rhs, xsend, own, xrecv, weave, zsend,
    local_sem, ar_send, ar_recv, pair_send, pair_recv, x_send, x_recv, z_send, z_recv, self_sem,
):
    nz = min(16, nb)
    ny = nb // nz
    tile = lax.axis_index("tile")
    beam = lax.axis_index("beam")
    core = lax.rem(tile, 2)
    chip_x = tile // 2
    partner = tile + 1 - 2 * core
    my_y = beam // nz
    my_z = lax.rem(beam, nz)
    chans = echo.shape[2]
    chunks = zsend.shape[0]
    slots = perm.shape[2]
    rows_total = steer.shape[1]
    blocks = rows_total // LANES
    half_blocks = slots // LANES
    nlane = chans // LANES

    def plane_peer(i):
        k = (nb - 1 - i) // ny
        dy = lax.rem(nb - 1 - i, ny)
        sign = 1 - 2 * lax.rem(k + 1, 2)
        dz = sign * ((k + 1) // 2)
        return lax.rem(my_y + dy, ny) * nz + lax.rem(my_z + dz + nz, nz)

    get_echo = pltpu.make_async_copy(echo_hbm, echo.at[core], local_sem.at[0])
    get_steer = pltpu.make_async_copy(steer_hbm, steer, local_sem.at[1])
    get_echo.start()
    get_steer.start()

    barrier = pltpu.get_barrier_semaphore()

    @pl.loop(0, nb - 1)
    def _(i):
        pl.semaphore_signal(barrier, inc=1, device_id={"beam": plane_peer(i)}, device_id_type=MESH)

    x_peers = [2 * lax.rem(chip_x + d, 4) + core for d in (2, 1, 3)]
    for peer in x_peers + [partner]:
        pl.semaphore_signal(barrier, inc=1, device_id={"tile": peer}, device_id_type=MESH)

    order_cols = order_ref[...].astype(F32)
    lane = lax.broadcasted_iota(jnp.int32, (LANES, LANES), 1)
    for b in range(blocks):
        cols[b] = jnp.broadcast_to(order_cols[b : b + 1, :], (LANES, LANES)).T

    get_echo.wait()
    for v in range(nlane):
        total = jnp.zeros((LANES, LANES), F32)
        for c in range(2):
            for q in range(chunks):
                part = echo[core, c, v * LANES : (v + 1) * LANES, q * LANES : (q + 1) * LANES].astype(F32)
                total = total + part * part
        power[beam, v : v + 1, :] = jnp.sum(total.T, axis=0, keepdims=True)

    lane_f = lane.astype(F32)

    def one_hot_block(b):
        col = cols[b]
        return [(col == lane_f + float(w * LANES)) for w in range(blocks)]

    def permuted(b):
        hot = jnp.concatenate([m.astype(F32).astype(BF16) for m in one_hot_block(b)], axis=1)
        left = jnp.dot(hot, steer[0], preferred_element_type=F32)
        right = jnp.dot(hot, steer[1], preferred_element_type=F32)
        return left.astype(BF16), right.astype(BF16)

    for u in range(half_blocks):
        masks = one_hot_block(tile * half_blocks + u)
        length = jnp.zeros((LANES, LANES), F32)
        keep = jnp.zeros((LANES, LANES), F32)
        for w in range(blocks):
            length = length + jnp.where(masks[w], lens_ref[w : w + 1, :].astype(F32), 0.0)
            keep = keep + jnp.where(masks[w], dwell_ref[w : w + 1, :].astype(F32), 0.0)
        length = jnp.sum(length, axis=1, keepdims=True)
        keep = jnp.sum(keep, axis=1, keepdims=True)
        gate = lax.rem(lane, G).astype(F32)
        limit[u * LANES : (u + 1) * LANES, :] = jnp.minimum(jnp.broadcast_to(length, (LANES, LANES)), G - gate)
        first = (lane // G + beam * (chunks * (LANES // G))).astype(F32)
        pulses[u * LANES : (u + 1) * LANES, :] = jnp.broadcast_to(keep, (LANES, LANES)) - first

    get_steer.wait()

    @pl.loop(0, 4 * half_blocks)
    def _(i):
        dest = i // half_blocks
        u = lax.rem(i, half_blocks)
        left, right = permuted((dest * 2 + core) * half_blocks + u)
        perm[core, dest, pl.ds(pl.multiple_of(u * LANES, LANES), LANES), :chans] = left
        perm[core, dest, pl.ds(pl.multiple_of(u * LANES, LANES), LANES), chans:] = right

    pl.semaphore_wait(barrier, nb - 1 + 4)

    @pl.loop(0, nb - 1)
    def _(i):
        pltpu.make_async_remote_copy(
            power.at[beam], power.at[beam], ar_send, ar_recv,
            device_id={"beam": plane_peer(i)}, device_id_type=MESH,
        ).start()

    send_echo = pltpu.make_async_remote_copy(
        echo.at[core], echo.at[core], pair_send.at[0], pair_recv.at[0],
        device_id={"tile": partner}, device_id_type=MESH,
    )
    send_echo.start()

    @pl.loop(0, 4 * half_blocks)
    def _(i):
        dest = i // half_blocks
        u = lax.rem(i, half_blocks)
        left, right = permuted((dest * 2 + 1 - core) * half_blocks + u)
        perm_out[dest, pl.ds(pl.multiple_of(u * LANES, LANES), LANES), :chans] = left
        perm_out[dest, pl.ds(pl.multiple_of(u * LANES, LANES), LANES), chans:] = right

    send_perm = pltpu.make_async_remote_copy(
        perm_out, perm.at[core], pair_send.at[1], pair_recv.at[1],
        device_id={"tile": partner}, device_id_type=MESH,
    )
    send_perm.start()

    everyone = power.at[pl.ds(0, nb - 1)]
    pltpu.make_async_copy(everyone, everyone, ar_recv).wait()
    summed = jnp.sum(power[...], axis=0)
    gains[core] = lax.rsqrt(summed * (1.0 / (nb * chunks * LANES)) + 1e-05)
    send_gain = pltpu.make_async_remote_copy(
        gains.at[core], gains.at[core], pair_send.at[2], pair_recv.at[2],
        device_id={"tile": partner}, device_id_type=MESH,
    )
    send_gain.start()

    def scale_side(side):
        for v in range(nlane):
            gain = jnp.broadcast_to(gains[side, v : v + 1, :], (LANES, LANES)).T
            top = slice(v * LANES, (v + 1) * LANES)
            low = slice(chans + v * LANES, chans + (v + 1) * LANES)
            for q in range(chunks):
                span = slice(q * LANES, (q + 1) * LANES)
                real = (echo[side, 0, top, span].astype(F32) * gain).astype(BF16)
                imag = (echo[side, 1, top, span].astype(F32) * gain).astype(BF16)
                rhs[q, side, top, :LANES] = real
                rhs[q, side, low, :LANES] = -imag
                rhs[q, side, top, LANES:] = imag
                rhs[q, side, low, LANES:] = real

    scale_side(core)
    send_echo.wait_recv()
    send_gain.wait_recv()
    scale_side(1 - core)
    send_perm.wait_recv()

    def partial_beams(q, dest):
        return jnp.dot(perm[0, dest], rhs[q, 0], preferred_element_type=F32) + jnp.dot(
            perm[1, dest], rhs[q, 1], preferred_element_type=F32
        )

    x_copies = []
    for q in range(chunks):
        for s, peer in enumerate(x_peers):
            xsend[q, s] = partial_beams(q, peer // 2).astype(BF16)
            copy = pltpu.make_async_remote_copy(
                xsend.at[q, s], xrecv.at[q, s], x_send.at[q, s], x_recv.at[q, s],
                device_id={"tile": peer}, device_id_type=MESH,
            )
            copy.start()
            x_copies.append(copy)
        own[q] = partial_beams(q, chip_x)

    step = 64
    for q in range(chunks):
        for s in range(3):
            x_copies[3 * q + s].wait_recv()

        @pl.loop(0, slots // step)
        def _(r):
            rows = pl.ds(pl.multiple_of(r * step, step), step)
            both = own[q, rows, :]
            for s in range(3):
                both = both + xrecv[q, s, rows, :].astype(F32)
            real, imag = both[:, :LANES], both[:, LANES:]
            cut = limit[rows, :]
            out_re = jnp.zeros((step, LANES), F32)
            out_im = jnp.zeros((step, LANES), F32)
            for tap in range(TAPS):
                live = cut > float(tap)
                shift_re = real if tap == 0 else pltpu.roll(real, LANES - tap, 1)
                shift_im = imag if tap == 0 else pltpu.roll(imag, LANES - tap, 1)
                shift_re = jnp.where(live, shift_re, 0.0)
                shift_im = jnp.where(live, shift_im, 0.0)
                code_re = code_ref[0, tap]
                code_im = code_ref[1, tap]
                out_re = out_re + (code_re * shift_re + code_im * shift_im)
                out_im = out_im + (code_re * shift_im - code_im * shift_re)
            kept = pulses[rows, :] > float(q * (LANES // G))
            weave[pl.ds(r * (2 * step), step, stride=2), :] = jnp.where(kept, out_re, 0.0)
            weave[pl.ds(r * (2 * step) + 1, step, stride=2), :] = jnp.where(kept, out_im, 0.0)

        zsend[q] = weave[...].reshape(zsend.shape[1:]).astype(BF16)

        @pl.loop(0, nb - 1)
        def _(i):
            peer = plane_peer(i)
            pltpu.make_async_remote_copy(
                zsend.at[q, peer], out_ref.at[q, beam], z_send.at[q], z_recv.at[q],
                device_id={"beam": peer}, device_id_type=MESH,
            ).start()

        pltpu.make_async_copy(zsend.at[q, beam], out_ref.at[q, beam], self_sem.at[q]).start()

    for q in range(chunks):
        arrived = out_ref.at[q, pl.ds(0, nb - 1)]
        pltpu.make_async_copy(arrived, arrived, z_recv.at[q]).wait()
        pltpu.make_async_copy(zsend.at[q, beam], out_ref.at[q, beam], self_sem.at[q]).wait()

    pltpu.make_async_copy(everyone, everyone, ar_send).wait()
    send_echo.wait_send()
    send_perm.wait_send()
    send_gain.wait_send()
    for copy in x_copies:
        copy.wait_send()
    for q in range(chunks):
        sent = zsend.at[q, pl.ds(0, nb - 1)]
        pltpu.make_async_copy(sent, sent, z_send.at[q]).wait()


def exchange(nb, echoes, steer, code, beam_order, dwell, code_len):
    chans, columns = echoes.shape[1], echoes.shape[2]
    total = steer.shape[1]
    slots = total // 8
    chunks = columns // LANES
    rows = 2 * slots // nb
    blocks = total // LANES
    vmem = pl.BlockSpec(memory_space=pltpu.VMEM)
    hbm = pl.BlockSpec(memory_space=pl.ANY)
    dma = pltpu.SemaphoreType.DMA

    def body(*refs):
        exchange_kernel(nb, *refs)

    return pl.pallas_call(
        body,
        out_shape=jax.ShapeDtypeStruct((chunks, nb, rows, LANES), BF16),
        in_specs=[hbm, hbm, vmem, vmem, vmem, pl.BlockSpec(memory_space=pltpu.SMEM)],
        out_specs=vmem,
        scratch_shapes=[
            pltpu.VMEM((2, 2, chans, columns), BF16),
            pltpu.VMEM(steer.shape, BF16),
            pltpu.VMEM((blocks, LANES, LANES), F32),
            pltpu.VMEM((2, 4, slots, 2 * chans), BF16),
            pltpu.VMEM((4, slots, 2 * chans), BF16),
            pltpu.VMEM((nb, chans // LANES, LANES), F32),
            pltpu.VMEM((2, chans // LANES, LANES), F32),
            pltpu.VMEM((slots, LANES), F32),
            pltpu.VMEM((slots, LANES), F32),
            pltpu.VMEM((chunks, 2, 2 * chans, 2 * LANES), BF16),
            pltpu.VMEM((chunks, 3, slots, 2 * LANES), BF16),
            pltpu.VMEM((chunks, slots, 2 * LANES), F32),
            pltpu.VMEM((chunks, 3, slots, 2 * LANES), BF16),
            pltpu.VMEM((2 * slots, LANES), F32),
            pltpu.VMEM((chunks, nb, rows, LANES), BF16),
            dma((2,)), dma, dma, dma((3,)), dma((3,)),
            dma((chunks, 3)), dma((chunks, 3)), dma((chunks,)), dma((chunks,)), dma((chunks,)),
        ],
        compiler_params=pltpu.CompilerParams(
            collective_id=0, has_side_effects=True, vmem_limit_bytes=40 << 20
        ),
        name="exchange",
    )(
        echoes, steer,
        beam_order.reshape(blocks, LANES), dwell.reshape(blocks, LANES), code_len.reshape(blocks, LANES),
        code.astype(F32),
    )


def dft_tables(nb, chunks, pulses_all):
    length = nb * chunks
    radix = pulses_all // length
    index = (np.arange(nb)[None, :] * chunks + np.arange(chunks)[:, None]).reshape(-1)
    angle = -2.0 * np.pi * ((index[:, None] * np.arange(length)[None, :]) % length) / length
    real, imag = np.cos(angle), np.sin(angle)
    table = np.block([[real, imag], [-imag, real]])
    turn = -2.0 * np.pi * np.arange(radix)[:, None] * np.arange(length)[None, :] / pulses_all
    twist = np.concatenate([np.cos(turn), np.sin(turn)], axis=0) / math.sqrt(pulses_all)
    return jnp.asarray(table, BF16), jnp.asarray(twist, F32)


def dft_kernel(x_ref, table_ref, twist_ref, out_ref, wide):
    chunks, nb, rows, _ = x_ref.shape
    length = chunks * nb
    wide[...] = x_ref[...].astype(F32).reshape(wide.shape)
    for slot in range(rows // 2):
        real = wide[pl.ds(2 * slot, length, stride=rows), :].T.astype(BF16)
        imag = wide[pl.ds(2 * slot + 1, length, stride=rows), :].T.astype(BF16)
        left = jnp.concatenate([real, imag], axis=1)
        found = jnp.dot(left, table_ref[...], preferred_element_type=F32)
        re, im = [], []
        for p in range(4):
            fr = found[p * G : (p + 1) * G, :length]
            fi = found[p * G : (p + 1) * G, length:]
            wr = twist_ref[p : p + 1, :]
            wi = twist_ref[4 + p : 5 + p, :]
            re.append(fr * wr - fi * wi)
            im.append(fr * wi + fi * wr)
        even_re, even_im = re[0] + re[2], im[0] + im[2]
        odd_re, odd_im = re[0] - re[2], im[0] - im[2]
        side_re, side_im = re[1] + re[3], im[1] + im[3]
        turn_re, turn_im = re[1] - re[3], im[1] - im[3]
        parts = [
            (even_re + side_re, even_im + side_im),
            (odd_re + turn_im, odd_im - turn_re),
            (even_re - side_re, even_im - side_im),
            (odd_re - turn_im, odd_im + turn_re),
        ]
        for k, (a, b) in enumerate(parts):
            out_ref[slot, 0, :, k * length : (k + 1) * length] = a
            out_ref[slot, 1, :, k * length : (k + 1) * length] = b


def doppler(x, pulses_all):
    chunks, nb, rows, _ = x.shape
    table, twist = dft_tables(nb, chunks, pulses_all)
    vmem = pl.BlockSpec(memory_space=pltpu.VMEM)
    return pl.pallas_call(
        dft_kernel,
        out_shape=jax.ShapeDtypeStruct((rows // 2, 2, G, pulses_all), F32),
        in_specs=[vmem, vmem, vmem],
        out_specs=vmem,
        scratch_shapes=[pltpu.VMEM((chunks * nb * rows, LANES), F32)],
        name="doppler",
    )(x, table, twist)


def solution(mesh):
    nb = mesh.shape["beam"]

    def on_device(echoes, steer, code, beam_order, dwell, code_len):
        arrived = exchange(nb, echoes, steer, code, beam_order, dwell, code_len)
        return doppler(arrived, nb * echoes.shape[2] // G)

    placed = (P(None, "tile", "beam"), P(None, None, "tile"), P(), P(), P(), P())
    return jax.shard_map(
        on_device,
        mesh=mesh,
        in_specs=placed,
        out_specs=P(("tile", "beam"), None, None, None),
        check_vma=False,
    )
```

time: 229 us -> 74.7 us (0.33)
  waiting for transfers between devices: 75.8 us -> 0 us
  Pallas kernels: 0 us -> 67.5 us
  local copies, waits for them, and re-layouts: 55.9 us -> 5.5 us
  starting transfers between devices: 38.7 us -> 0 us
  other arithmetic: 30.9 us -> 0.66 us
  matrix products: 26.1 us -> 0 us
    all_to_all x3 -> x0, waiting for transfers between devices: 75.8 us -> none  [the longest x1 44.9 us: sum_at_owner(): lax.all_to_all(pieces, axis, split_axis=0, concat_axis=0, tiled=True)]
    pallas_call x0 -> x2, Pallas kernels: none -> 67.5 us  [the longest x1 64.7 us: exchange(): pl.pallas_call(body, out_shape=jax.ShapeDtypeStruct((chunks, nb, rows, LA...]
    all_to_all x3 -> x0, starting transfers between devices: 38.7 us -> none  [the longest x1 18.7 us: copy_for_each(): lax.all_to_all(jnp.broadcast_to(x[None], (count, *x.shape)), axis, 0, 0,...]
    dot_general x9 -> x0, matrix products: 26.1 us -> none  [the longest x8 23.8 us: highest(): return jnp.einsum(form, left, right, precision=lax.Precision.HIGHEST)]
    gather x3 -> x0, local copies, waits for them, and re-layouts: 23.5 us -> none  [the longest x1 20 us: on_device(): ordered = jnp.take(steer, beam_order, axis=1)]
    add x3 -> x0, other arithmetic: 21.9 us -> none  [the longest x1 11 us: compress(): out_im = out_im + live * (code_re[tap] * shift_im - code_im[tap] * shift_re)]
    reduce_sum x3 -> x0, other arithmetic: 5.19 us -> none  [the longest x1 3.72 us: sum_at_owner(): return arrived.astype(jnp.float32).sum(axis=0)]
    another operation x2 -> x0, local copies, waits for them, and re-layouts: 4.87 us -> none  [on_device(): jnp.stack([final_re, final_im], axis=1)]
  transfers between devices with their start and end apart: 3 -> 0, of which waited for: 2 -> 0; matrix products, arithmetic and copies ran while one was open for 11% -> 0% of each run, Pallas kernels for 0% -> 0%
where the time goes in v1:
time: 74.7 us; the launch traced here: 73.7 us
  Pallas kernels  67.5 us (90%)
  local copies, waits for them, and re-layouts  5.5 us (7%)
    pallas_call x1, Pallas kernels, exchange(): pl.pallas_call(body, out_shape=jax.ShapeDtypeStruct((chunks, nb, rows, LA...  64.7 us
    unnamed x12, local copies, waits for them, and re-layouts  5.5 us
    pallas_call x1, Pallas kernels, doppler(): pl.pallas_call(dft_kernel, out_shape=jax.ShapeDtypeStruct((rows // 2, 2,...  2.8 us

profile of v1, /device:TPU:24, one launch (start us, length us, event | category | flops | bytes accessed | tf_op | source)
XLA Modules:
  0.0 73.7 jit_solution(4903724012172679975)
XLA Ops:
  0.0 0.7 convert_element_type.3.refs_5_
  0.7 0.0 copy-start
  0.7 1.6 %copy-done = bf16[2,2048,256]{2,1,0:T(8,128)(2,1)S(1)} copy-done((bf16[2,2048,256]{2,1,0:T(8,128)(2,1)S(1)}, bf16[2,2048,256]{2,1,0:T(8,128)(2,1)}, u32[]{:S(2)}) %copy-start) | copy-done | bytes 2097176
  2.2 0.0 copy-start.2
  2.3 1.0 %copy-done.2 = bf16[2,256,512]{2,1,0:T(8,128)(2,1)S(1)} copy-done((bf16[2,256,512]{2,1,0:T(8,128)(2,1)S(1)}, bf16[2,256,512]{2,1,0:T(8,128)(2,1)}, u32[]{:S(2)}) %copy-start.2) | copy-done | bytes 524312
  3.3 0.0 copy-start.3
  3.3 0.7 copy-done.3
  4.0 0.0 copy-start.4
  4.0 0.7 copy-done.4
  4.7 0.0 copy-start.5
  4.7 0.7 copy-done.5
  5.4 64.7 %exchange.1.x_ref = bf16[4,64,8,128]{3,2,1,0:T(8,128)(2,1)S(1)} custom-call(bf16[2,256,512]{2,1,0:T(8,128)(2,1)S(1)} %copy-done.2, bf16[2,2048,256]{2,1,0:T(8,128)(2,1)S(1)} %copy-done, s32[16,128]{1,0:T(8,128)S(1)} %bitcast.3, s32[16,128]{1,0:T(8,128)S(1)} %bitcast.4, s32[16,128]{1,0:T(8,128)S(1)} %bitcast.5, f32[2,8]{1,0:T(2,128)S(1)} %convert_element_type.3.refs_5_), custom_call_target="tpu_custom_call" | custom-call | tf_op jit(solution)/shard_map/exchange/pallas_call | solution.py:262
  70.1 0.0 copy-start.1
  70.1 0.8 %copy-done.1 = bf16[4,64,8,128]{3,2,1,0:T(8,128)(2,1)} copy-done((bf16[4,64,8,128]{3,2,1,0:T(8,128)(2,1)}, bf16[4,64,8,128]{3,2,1,0:T(8,128)(2,1)S(1)}, u32[]{:S(2)}) %copy-start.1) | copy-done | bytes 524312
  70.9 2.8 %doppler.1 = f32[4,2,32,1024]{3,2,1,0:T(8,128)} custom-call(bf16[4,64,8,128]{3,2,1,0:T(8,128)(2,1)} %copy-done.1, bf16[512,512]{1,0:T(8,128)(2,1)} %constant.4.clone.table_ref, f32[8,256]{1,0:T(8,128)} %constant.5.clone.twist_ref), custom_call_target="tpu_custom_call" | custom-call | tf_op jit(solution)/shard_map/doppler/pallas_call | solution.py:345
Async XLA Ops:
  0.7 1.6 %copy-start = (bf16[2,2048,256]{2,1,0:T(8,128)(2,1)S(1)}, bf16[2,2048,256]{2,1,0:T(8,128)(2,1)}, u32[]{:S(2)}) copy-start(bf16[2,2048,256]{2,1,0:T(8,128)(2,1)} %refs_1_.1) | copy-start | bytes 6291460
  2.2 1.0 %copy-start.2 = (bf16[2,256,512]{2,1,0:T(8,128)(2,1)S(1)}, bf16[2,256,512]{2,1,0:T(8,128)(2,1)}, u32[]{:S(2)}) copy-start(bf16[2,256,512]{2,1,0:T(8,128)(2,1)} %refs_0_.1) | copy-start | bytes 1572868
  3.3 0.7 copy-start.3
  4.0 0.7 copy-start.4
  4.7 0.7 copy-start.5
  70.1 0.8 %copy-start.1 = (bf16[4,64,8,128]{3,2,1,0:T(8,128)(2,1)}, bf16[4,64,8,128]{3,2,1,0:T(8,128)(2,1)S(1)}, u32[]{:S(2)}) copy-start(bf16[4,64,8,128]{3,2,1,0:T(8,128)(2,1)S(1)} %exchange.1.x_ref) | copy-start | bytes 1572868

commit v2 on v1

--- a/solution.py
+++ b/solution.py
@@ -18,8 +18,9 @@
 
 def exchange_kernel(
     nb,
-    echo_hbm, steer_hbm, order_ref, dwell_ref, lens_ref, code_ref,
+    echo_hbm, steer_hbm, order_hbm, dwell_hbm, lens_hbm, code_hbm,
     out_ref,
+    order_ref, dwell_ref, lens_ref, code_ref, coef,
     echo, steer, cols, perm, perm_out, power, gains, limit, pulses, rhs, xsend, own, xrecv, weave, zsend,
     local_sem, ar_send, ar_recv, pair_send, pair_recv, x_send, x_recv, z_send, z_recv, self_sem,
 ):
@@ -49,8 +50,18 @@
 
     get_echo = pltpu.make_async_copy(echo_hbm, echo.at[core], local_sem.at[0])
     get_steer = pltpu.make_async_copy(steer_hbm, steer, local_sem.at[1])
+    small = [
+        pltpu.make_async_copy(source, target, local_sem.at[2 + n])
+        for n, (source, target) in enumerate(
+            [(order_hbm, order_ref), (dwell_hbm, dwell_ref), (lens_hbm, lens_ref), (code_hbm, code_ref)]
+        )
+    ]
+    for copy in small[:1]:
+        copy.start()
     get_echo.start()
     get_steer.start()
+    for copy in small[1:]:
+        copy.start()
 
     barrier = pltpu.get_barrier_semaphore()
 
@@ -62,6 +73,7 @@
     for peer in x_peers + [partner]:
         pl.semaphore_signal(barrier, inc=1, device_id={"tile": peer}, device_id_type=MESH)
 
+    small[0].wait()
     order_cols = order_ref[...].astype(F32)
     lane = lax.broadcasted_iota(jnp.int32, (LANES, LANES), 1)
     for b in range(blocks):
@@ -87,6 +99,13 @@
         left = jnp.dot(hot, steer[0], preferred_element_type=F32)
         right = jnp.dot(hot, steer[1], preferred_element_type=F32)
         return left.astype(BF16), right.astype(BF16)
+
+    for copy in small[1:]:
+        copy.wait()
+    taps = code_ref[...].astype(F32)
+    for tap in range(TAPS):
+        for c in range(2):
+            coef[2 * tap + c] = jnp.broadcast_to(taps[c : c + 1, tap : tap + 1], coef.shape[1:])
 
     for u in range(half_blocks):
         masks = one_hot_block(tile * half_blocks + u)
@@ -199,23 +218,24 @@
             both = own[q, rows, :]
             for s in range(3):
                 both = both + xrecv[q, s, rows, :].astype(F32)
-            real, imag = both[:, :LANES], both[:, LANES:]
-            cut = limit[rows, :]
-            out_re = jnp.zeros((step, LANES), F32)
-            out_im = jnp.zeros((step, LANES), F32)
+            tiled = (step // 8, 8, LANES)
+            real, imag = both[:, :LANES].reshape(tiled), both[:, LANES:].reshape(tiled)
+            cut = limit[rows, :].reshape(tiled)
+            out_re = jnp.zeros(tiled, F32)
+            out_im = jnp.zeros(tiled, F32)
             for tap in range(TAPS):
                 live = cut > float(tap)
-                shift_re = real if tap == 0 else pltpu.roll(real, LANES - tap, 1)
-                shift_im = imag if tap == 0 else pltpu.roll(imag, LANES - tap, 1)
+                shift_re = real if tap == 0 else pltpu.roll(real, LANES - tap, 2)
+                shift_im = imag if tap == 0 else pltpu.roll(imag, LANES - tap, 2)
                 shift_re = jnp.where(live, shift_re, 0.0)
                 shift_im = jnp.where(live, shift_im, 0.0)
-                code_re = code_ref[0, tap]
-                code_im = code_ref[1, tap]
+                code_re = coef[2 * tap]
+                code_im = coef[2 * tap + 1]
                 out_re = out_re + (code_re * shift_re + code_im * shift_im)
                 out_im = out_im + (code_re * shift_im - code_im * shift_re)
-            kept = pulses[rows, :] > float(q * (LANES // G))
-            weave[pl.ds(r * (2 * step), step, stride=2), :] = jnp.where(kept, out_re, 0.0)
-            weave[pl.ds(r * (2 * step) + 1, step, stride=2), :] = jnp.where(kept, out_im, 0.0)
+            kept = pulses[rows, :].reshape(tiled) > float(q * (LANES // G))
+            weave[pl.ds(r * (2 * step), step, stride=2), :] = jnp.where(kept, out_re, 0.0).reshape(step, LANES)
+            weave[pl.ds(r * (2 * step) + 1, step, stride=2), :] = jnp.where(kept, out_im, 0.0).reshape(step, LANES)
 
         zsend[q] = weave[...].reshape(zsend.shape[1:]).astype(BF16)
 
@@ -253,7 +273,7 @@
     rows = 2 * slots // nb
     blocks = total // LANES
     vmem = pl.BlockSpec(memory_space=pltpu.VMEM)
-    hbm = pl.BlockSpec(memory_space=pl.ANY)
+    hbm = pl.BlockSpec(memory_space=pltpu.HBM)
     dma = pltpu.SemaphoreType.DMA
 
     def body(*refs):
@@ -262,9 +282,14 @@
     return pl.pallas_call(
         body,
         out_shape=jax.ShapeDtypeStruct((chunks, nb, rows, LANES), BF16),
-        in_specs=[hbm, hbm, vmem, vmem, vmem, pl.BlockSpec(memory_space=pltpu.SMEM)],
+        in_specs=[hbm] * 6,
         out_specs=vmem,
         scratch_shapes=[
+            pltpu.VMEM((blocks, LANES), jnp.int32),
+            pltpu.VMEM((blocks, LANES), jnp.int32),
+            pltpu.VMEM((blocks, LANES), jnp.int32),
+            pltpu.VMEM(code.shape, BF16),
+            pltpu.VMEM((2 * TAPS, 8, LANES), F32),
             pltpu.VMEM((2, 2, chans, columns), BF16),
             pltpu.VMEM(steer.shape, BF16),
             pltpu.VMEM((blocks, LANES, LANES), F32),
@@ -280,7 +305,7 @@
             pltpu.VMEM((chunks, 3, slots, 2 * LANES), BF16),
             pltpu.VMEM((2 * slots, LANES), F32),
             pltpu.VMEM((chunks, nb, rows, LANES), BF16),
-            dma((2,)), dma, dma, dma((3,)), dma((3,)),
+            dma((6,)), dma, dma, dma((3,)), dma((3,)),
             dma((chunks, 3)), dma((chunks, 3)), dma((chunks,)), dma((chunks,)), dma((chunks,)),
         ],
         compiler_params=pltpu.CompilerParams(
@@ -288,9 +313,14 @@
         ),
         name="exchange",
     )(
-        echoes, steer,
-        beam_order.reshape(blocks, LANES), dwell.reshape(blocks, LANES), code_len.reshape(blocks, LANES),
-        code.astype(F32),
+        *[
+            pltpu.with_memory_space_constraint(x, pltpu.HBM)
+            for x in (
+                echoes, steer,
+                beam_order.reshape(blocks, LANES), dwell.reshape(blocks, LANES), code_len.reshape(blocks, LANES),
+                code,
+            )
+        ]
     )
 
 
@@ -309,33 +339,37 @@
 def dft_kernel(x_ref, table_ref, twist_ref, out_ref, wide):
     chunks, nb, rows, _ = x_ref.shape
     length = chunks * nb
-    wide[...] = x_ref[...].astype(F32).reshape(wide.shape)
-    for slot in range(rows // 2):
-        real = wide[pl.ds(2 * slot, length, stride=rows), :].T.astype(BF16)
-        imag = wide[pl.ds(2 * slot + 1, length, stride=rows), :].T.astype(BF16)
-        left = jnp.concatenate([real, imag], axis=1)
-        found = jnp.dot(left, table_ref[...], preferred_element_type=F32)
-        re, im = [], []
-        for p in range(4):
-            fr = found[p * G : (p + 1) * G, :length]
-            fi = found[p * G : (p + 1) * G, length:]
-            wr = twist_ref[p : p + 1, :]
-            wi = twist_ref[4 + p : 5 + p, :]
-            re.append(fr * wr - fi * wi)
-            im.append(fr * wi + fi * wr)
-        even_re, even_im = re[0] + re[2], im[0] + im[2]
-        odd_re, odd_im = re[0] - re[2], im[0] - im[2]
-        side_re, side_im = re[1] + re[3], im[1] + im[3]
-        turn_re, turn_im = re[1] - re[3], im[1] - im[3]
-        parts = [
-            (even_re + side_re, even_im + side_im),
-            (odd_re + turn_im, odd_im - turn_re),
-            (even_re - side_re, even_im - side_im),
-            (odd_re - turn_im, odd_im + turn_re),
-        ]
-        for k, (a, b) in enumerate(parts):
-            out_ref[slot, 0, :, k * length : (k + 1) * length] = a
-            out_ref[slot, 1, :, k * length : (k + 1) * length] = b
+    slot = pl.program_id(0)
+
+    @pl.when(slot == 0)
+    def _():
+        wide[...] = x_ref[...].astype(F32).reshape(wide.shape)
+
+    real = wide[pl.ds(2 * slot, length, stride=rows), :].T.astype(BF16)
+    imag = wide[pl.ds(2 * slot + 1, length, stride=rows), :].T.astype(BF16)
+    left = jnp.concatenate([real, imag], axis=1)
+    found = jnp.dot(left, table_ref[...], preferred_element_type=F32)
+    re, im = [], []
+    for p in range(4):
+        fr = found[p * G : (p + 1) * G, :length]
+        fi = found[p * G : (p + 1) * G, length:]
+        wr = twist_ref[p : p + 1, :]
+        wi = twist_ref[4 + p : 5 + p, :]
+        re.append(fr * wr - fi * wi)
+        im.append(fr * wi + fi * wr)
+    even_re, even_im = re[0] + re[2], im[0] + im[2]
+    odd_re, odd_im = re[0] - re[2], im[0] - im[2]
+    side_re, side_im = re[1] + re[3], im[1] + im[3]
+    turn_re, turn_im = re[1] - re[3], im[1] - im[3]
+    parts = [
+        (even_re + side_re, even_im + side_im),
+        (odd_re + turn_im, odd_im - turn_re),
+        (even_re - side_re, even_im - side_im),
+        (odd_re - turn_im, odd_im + turn_re),
+    ]
+    for k, (a, b) in enumerate(parts):
+        out_ref[0, 0, :, k * length : (k + 1) * length] = a
+        out_ref[0, 1, :, k * length : (k + 1) * length] = b
 
 
 def doppler(x, pulses_all):
@@ -344,10 +378,12 @@
     vmem = pl.BlockSpec(memory_space=pltpu.VMEM)
     return pl.pallas_call(
         dft_kernel,
+        grid=(rows // 2,),
         out_shape=jax.ShapeDtypeStruct((rows // 2, 2, G, pulses_all), F32),
         in_specs=[vmem, vmem, vmem],
-        out_specs=vmem,
+        out_specs=pl.BlockSpec((1, 2, G, pulses_all), lambda n: (n, 0, 0, 0)),
         scratch_shapes=[pltpu.VMEM((chunks * nb * rows, LANES), F32)],
+        compiler_params=pltpu.CompilerParams(vmem_limit_bytes=8 << 20),
         name="doppler",
     )(x, table, twist)
 

time: 74.7 us -> 67.5 us (0.904)
  local copies, waits for them, and re-layouts: 5.5 us -> 0.01 us
  Pallas kernels: 67.5 us -> 66.7 us
    unnamed x12 -> x4, local copies, waits for them, and re-layouts: 5.5 us -> 0.01 us
where the time goes in v2:
time: 67.5 us; the launch traced here: 66.8 us
  Pallas kernels  66.7 us (99%)
    pallas_call x1, Pallas kernels, exchange(): pl.pallas_call(body, out_shape=jax.ShapeDtypeStruct((chunks, nb, rows, LA...  64.3 us
    pallas_call x1, Pallas kernels, doppler(): pl.pallas_call(dft_kernel, grid=(rows // 2,), out_shape=jax.ShapeDtypeStr...  2.43 us

profile of v2, /device:TPU:24, one launch (start us, length us, event | category | flops | bytes accessed | tf_op | source)
XLA Modules:
  0.0 66.8 jit_solution(3251410498032224794)
XLA Ops:
  0.0 0.0 copy-start.1
  0.0 0.0 copy-start
  0.0 64.3 %exchange.1.x_ref = bf16[4,64,8,128]{3,2,1,0:T(8,128)(2,1)S(1)} custom-call(bf16[2,256,512]{2,1,0:T(8,128)(2,1)} %refs_0_.1, bf16[2,2048,256]{2,1,0:T(8,128)(2,1)} %refs_1_.1, s32[16,128]{1,0:T(8,128)} %bitcast.3, s32[16,128]{1,0:T(8,128)} %bitcast.4, s32[16,128]{1,0:T(8,128)} %bitcast.5, bf16[2,8]{1,0:T(2,128)(2,1)} %refs_5_.1), custom_call_target="tpu_custom_call" | custom-call | tf_op jit(solution)/shard_map/exchange/pallas_call | solution.py:282
  64.3 0.0 copy-done.1
  64.3 0.0 copy-done
  64.3 2.4 %doppler.1 = f32[4,2,32,1024]{3,2,1,0:T(8,128)} custom-call(bf16[4,64,8,128]{3,2,1,0:T(8,128)(2,1)S(1)} %exchange.1.x_ref, bf16[512,512]{1,0:T(8,128)(2,1)S(1)} %copy-done, f32[8,256]{1,0:T(8,128)S(1)} %copy-done.1), custom_call_target="tpu_custom_call" | custom-call | tf_op jit(solution)/shard_map/doppler/pallas_call | solution.py:379
Async XLA Ops:
  0.0 64.3 %copy-start.1 = (f32[8,256]{1,0:T(8,128)S(1)}, f32[8,256]{1,0:T(8,128)}, u32[]{:S(2)}) copy-start(f32[8,256]{1,0:T(8,128)} %constant.5.clone.twist_ref) | copy-start | bytes 24580
  0.0 64.3 %copy-start = (bf16[512,512]{1,0:T(8,128)(2,1)S(1)}, bf16[512,512]{1,0:T(8,128)(2,1)}, u32[]{:S(2)}) copy-start(bf16[512,512]{1,0:T(8,128)(2,1)} %constant.4.clone.table_ref) | copy-start | bytes 1572868

commit v3 on v2

--- a/solution.py
+++ b/solution.py
@@ -21,8 +21,8 @@
     echo_hbm, steer_hbm, order_hbm, dwell_hbm, lens_hbm, code_hbm,
     out_ref,
     order_ref, dwell_ref, lens_ref, code_ref, coef,
-    echo, steer, cols, perm, perm_out, power, gains, limit, pulses, rhs, xsend, own, xrecv, weave, zsend,
-    local_sem, ar_send, ar_recv, pair_send, pair_recv, x_send, x_recv, z_send, z_recv, self_sem,
+    echo, steer, cols, perm, perm_out, power, stage, gathered, gains, spread, limit, pulses, rhs, far_out, far_in, near_out, near_in, hold, own, weave, zsend,
+    local_sem, ar_send, ar_recv, pair_send, pair_recv, far_send, far_recv, near_send, near_recv, z_send, z_recv, self_sem,
 ):
     nz = min(16, nb)
     ny = nb // nz
@@ -30,7 +30,6 @@
     beam = lax.axis_index("beam")
     core = lax.rem(tile, 2)
     chip_x = tile // 2
-    partner = tile + 1 - 2 * core
     my_y = beam // nz
     my_z = lax.rem(beam, nz)
     chans = echo.shape[2]
@@ -41,12 +40,33 @@
     half_blocks = slots // LANES
     nlane = chans // LANES
 
-    def plane_peer(i):
-        k = (nb - 1 - i) // ny
-        dy = lax.rem(nb - 1 - i, ny)
-        sign = 1 - 2 * lax.rem(k + 1, 2)
-        dz = sign * ((k + 1) // 2)
-        return lax.rem(my_y + dy, ny) * nz + lax.rem(my_z + dz + nz, nz)
+    other = 2 * chip_x + 1 - core
+    ys = [lax.rem(my_y + d, ny) for d in range(ny)]
+
+    def zs(d):
+        return lax.rem(my_z + (d + nz), nz)
+
+    def at(side, y, z):
+        return {"tile": side, "beam": y * nz + z}
+
+    def start_plane_sends(source, target, sent, received):
+        def send(y, z):
+            peer = y * nz + z
+            pltpu.make_async_remote_copy(
+                source(peer), target, sent, received, device_id={"beam": peer}, device_id_type=MESH
+            ).start()
+
+        for y in ys:
+            send(y, zs(nz // 2))
+
+        @pl.loop(1, nz // 2)
+        def _(m):
+            for z in (zs(nz // 2 + m - nz), zs(nz // 2 - m)):
+                for y in ys:
+                    send(y, z)
+
+        for y in ys[1:]:
+            send(y, my_z)
 
     get_echo = pltpu.make_async_copy(echo_hbm, echo.at[core], local_sem.at[0])
     get_steer = pltpu.make_async_copy(steer_hbm, steer, local_sem.at[1])
@@ -65,13 +85,13 @@
 
     barrier = pltpu.get_barrier_semaphore()
 
-    @pl.loop(0, nb - 1)
-    def _(i):
-        pl.semaphore_signal(barrier, inc=1, device_id={"beam": plane_peer(i)}, device_id_type=MESH)
-
-    x_peers = [2 * lax.rem(chip_x + d, 4) + core for d in (2, 1, 3)]
-    for peer in x_peers + [partner]:
-        pl.semaphore_signal(barrier, inc=1, device_id={"tile": peer}, device_id_type=MESH)
+    sides = [lax.rem(chip_x + d, 4) for d in (1, 3)]
+    greeted = [at(tile, my_y, zs(d)) for d in (-4, -3, -2, -1, 1, 2, 3, 4)]
+    greeted += [at(tile, y, zs(d)) for y in ys[1:] for d in (0, 4, -4)]
+    greeted += [at(other, y, zs(d)) for y in ys for d in (0, 4, -4)]
+    greeted += [{"tile": 2 * side + core} for side in sides]
+    for peer in greeted:
+        pl.semaphore_signal(barrier, inc=1, device_id=peer, device_id_type=MESH)
 
     small[0].wait()
     order_cols = order_ref[...].astype(F32)
@@ -86,7 +106,7 @@
             for q in range(chunks):
                 part = echo[core, c, v * LANES : (v + 1) * LANES, q * LANES : (q + 1) * LANES].astype(F32)
                 total = total + part * part
-        power[beam, v : v + 1, :] = jnp.sum(total.T, axis=0, keepdims=True)
+        power[4, v : v + 1, :] = jnp.sum(total.T, axis=0, keepdims=True)
 
     lane_f = lane.astype(F32)
 
@@ -99,6 +119,58 @@
         left = jnp.dot(hot, steer[0], preferred_element_type=F32)
         right = jnp.dot(hot, steer[1], preferred_element_type=F32)
         return left.astype(BF16), right.astype(BF16)
+
+    get_steer.wait()
+
+    def permute(target, side, first, last):
+        @pl.loop(first, last)
+        def _(i):
+            dest = i // half_blocks
+            u = lax.rem(i, half_blocks)
+            left, right = permuted((dest * 2 + side) * half_blocks + u)
+            rows = pl.ds(pl.multiple_of(u * LANES, LANES), LANES)
+            target[dest, rows, :chans] = left
+            target[dest, rows, chans:] = right
+
+    permute(perm_out, 1 - core, 0, 2 * half_blocks)
+    pl.semaphore_wait(barrier, len(greeted))
+
+    for d in (-4, 4, -3, 3, -2, 2, -1, 1):
+        pltpu.make_async_remote_copy(
+            power.at[4], power.at[4 - d], ar_send.at[0], ar_recv.at[0],
+            device_id=at(tile, my_y, zs(d)), device_id_type=MESH,
+        ).start()
+
+    send_echo = pltpu.make_async_remote_copy(
+        echo.at[core], echo.at[core], pair_send.at[0], pair_recv.at[0],
+        device_id={"tile": other}, device_id_type=MESH,
+    )
+    send_echo.start()
+    permute(perm_out, 1 - core, 2 * half_blocks, 4 * half_blocks)
+    send_perm = pltpu.make_async_remote_copy(
+        perm_out, perm.at[core], pair_send.at[1], pair_recv.at[1],
+        device_id={"tile": other}, device_id_type=MESH,
+    )
+    send_perm.start()
+    permute(perm.at[core], core, 0, 2 * half_blocks)
+
+    nearby = power.at[pl.ds(0, 8)]
+    pltpu.make_async_copy(nearby, nearby, ar_recv.at[0]).wait()
+    around = jnp.sum(power[...], axis=0)
+    stage[0] = around
+    stage[1] = jnp.sum(power[5:9], axis=0)
+    stage[2] = jnp.sum(power[1:4], axis=0)
+    gathered[(core * 3) * ny + my_y] = around
+    for kind, d in ((1, -4), (2, 4), (0, 0)):
+        for step, y in enumerate(ys):
+            for side in (tile, other):
+                if kind == 0 and step == 0 and side is tile:
+                    continue
+                pltpu.make_async_remote_copy(
+                    stage.at[kind], gathered.at[(core * 3 + kind) * ny + my_y], ar_send.at[1], ar_recv.at[1],
+                    device_id=at(side, y, zs(d)), device_id_type=MESH,
+                ).start()
+    permute(perm.at[core], core, 2 * half_blocks, 4 * half_blocks)
 
     for copy in small[1:]:
         copy.wait()
@@ -121,103 +193,104 @@
         first = (lane // G + beam * (chunks * (LANES // G))).astype(F32)
         pulses[u * LANES : (u + 1) * LANES, :] = jnp.broadcast_to(keep, (LANES, LANES)) - first
 
-    get_steer.wait()
-
-    @pl.loop(0, 4 * half_blocks)
-    def _(i):
-        dest = i // half_blocks
-        u = lax.rem(i, half_blocks)
-        left, right = permuted((dest * 2 + core) * half_blocks + u)
-        perm[core, dest, pl.ds(pl.multiple_of(u * LANES, LANES), LANES), :chans] = left
-        perm[core, dest, pl.ds(pl.multiple_of(u * LANES, LANES), LANES), chans:] = right
-
-    pl.semaphore_wait(barrier, nb - 1 + 4)
-
-    @pl.loop(0, nb - 1)
-    def _(i):
-        pltpu.make_async_remote_copy(
-            power.at[beam], power.at[beam], ar_send, ar_recv,
-            device_id={"beam": plane_peer(i)}, device_id_type=MESH,
-        ).start()
-
-    send_echo = pltpu.make_async_remote_copy(
-        echo.at[core], echo.at[core], pair_send.at[0], pair_recv.at[0],
-        device_id={"tile": partner}, device_id_type=MESH,
-    )
-    send_echo.start()
-
-    @pl.loop(0, 4 * half_blocks)
-    def _(i):
-        dest = i // half_blocks
-        u = lax.rem(i, half_blocks)
-        left, right = permuted((dest * 2 + 1 - core) * half_blocks + u)
-        perm_out[dest, pl.ds(pl.multiple_of(u * LANES, LANES), LANES), :chans] = left
-        perm_out[dest, pl.ds(pl.multiple_of(u * LANES, LANES), LANES), chans:] = right
-
-    send_perm = pltpu.make_async_remote_copy(
-        perm_out, perm.at[core], pair_send.at[1], pair_recv.at[1],
-        device_id={"tile": partner}, device_id_type=MESH,
-    )
-    send_perm.start()
-
-    everyone = power.at[pl.ds(0, nb - 1)]
-    pltpu.make_async_copy(everyone, everyone, ar_recv).wait()
-    summed = jnp.sum(power[...], axis=0)
-    gains[core] = lax.rsqrt(summed * (1.0 / (nb * chunks * LANES)) + 1e-05)
-    send_gain = pltpu.make_async_remote_copy(
-        gains.at[core], gains.at[core], pair_send.at[2], pair_recv.at[2],
-        device_id={"tile": partner}, device_id_type=MESH,
-    )
-    send_gain.start()
-
-    def scale_side(side):
+    everyone = gathered.at[pl.ds(0, 6 * ny - 1)]
+    pltpu.make_async_copy(everyone, everyone, ar_recv.at[1]).wait()
+    for side in range(2):
+        total = jnp.sum(gathered[side * 3 * ny : (side + 1) * 3 * ny], axis=0)
+        gains[side] = lax.rsqrt(total * (1.0 / (nb * chunks * LANES)) + 1e-05)
+
+    def spread_gain(side):
         for v in range(nlane):
-            gain = jnp.broadcast_to(gains[side, v : v + 1, :], (LANES, LANES)).T
+            spread[side, v] = jnp.broadcast_to(gains[side, v : v + 1, :], (LANES, LANES)).T
+
+    def scale(side, q):
+        for v in range(nlane):
+            gain = spread[side, v]
             top = slice(v * LANES, (v + 1) * LANES)
             low = slice(chans + v * LANES, chans + (v + 1) * LANES)
-            for q in range(chunks):
-                span = slice(q * LANES, (q + 1) * LANES)
-                real = (echo[side, 0, top, span].astype(F32) * gain).astype(BF16)
-                imag = (echo[side, 1, top, span].astype(F32) * gain).astype(BF16)
-                rhs[q, side, top, :LANES] = real
-                rhs[q, side, low, :LANES] = -imag
-                rhs[q, side, top, LANES:] = imag
-                rhs[q, side, low, LANES:] = real
-
-    scale_side(core)
+            span = slice(q * LANES, (q + 1) * LANES)
+            real = (echo[side, 0, top, span].astype(F32) * gain).astype(BF16)
+            imag = (echo[side, 1, top, span].astype(F32) * gain).astype(BF16)
+            rhs[q, side, top, :LANES] = real
+            rhs[q, side, low, :LANES] = -imag
+            rhs[q, side, top, LANES:] = imag
+            rhs[q, side, low, LANES:] = real
+
     send_echo.wait_recv()
-    send_gain.wait_recv()
-    scale_side(1 - core)
     send_perm.wait_recv()
+    spread_gain(0)
+    spread_gain(1)
 
     def partial_beams(q, dest):
         return jnp.dot(perm[0, dest], rhs[q, 0], preferred_element_type=F32) + jnp.dot(
             perm[1, dest], rhs[q, 1], preferred_element_type=F32
         )
 
+    half = slots // 2
+    direct = [slice(half, slots), slice(0, half)]
+    summed = [slice(0, half), slice(half, slots)]
     x_copies = []
-    for q in range(chunks):
-        for s, peer in enumerate(x_peers):
-            xsend[q, s] = partial_beams(q, peer // 2).astype(BF16)
-            copy = pltpu.make_async_remote_copy(
-                xsend.at[q, s], xrecv.at[q, s], x_send.at[q, s], x_recv.at[q, s],
-                device_id={"tile": peer}, device_id_type=MESH,
+
+    def to_side(side, source, target, sent, received):
+        copy = pltpu.make_async_remote_copy(
+            source, target, sent, received,
+            device_id={"tile": 2 * sides[side] + core}, device_id_type=MESH,
+        )
+        copy.start()
+        x_copies.append(copy)
+        return copy
+
+    far, near = {}, {}
+
+    def form(q):
+        scale(0, q)
+        scale(1, q)
+        product = partial_beams(q, lax.rem(chip_x + 2, 4))
+        for side in range(2):
+            far_out[q, side] = product[summed[side]].astype(BF16)
+        for side in range(2):
+            product = partial_beams(q, sides[side])
+            near_out[q, side, direct[side]] = product[direct[side]].astype(BF16)
+            hold[q, side] = product[summed[side]]
+        own[q] = partial_beams(q, chip_x)
+
+    def start_far(q):
+        for side in range(2):
+            far[q, side] = to_side(
+                side, far_out.at[q, side], far_in.at[q, side], far_send.at[q, side], far_recv.at[q, side]
             )
-            copy.start()
-            x_copies.append(copy)
-        own[q] = partial_beams(q, chip_x)
+
+    def start_near(q):
+        for side in range(2):
+            part = direct[side]
+            near[q, side, 0] = to_side(
+                side, near_out.at[q, side, part], near_in.at[q, side, part],
+                near_send.at[q, side, 0], near_recv.at[q, side, 0],
+            )
+
+    def relay(q):
+        for side in range(2):
+            far[q, side].wait_recv()
+            part = summed[side]
+            near_out[q, side, part] = (hold[q, side] + far_in[q, side].astype(F32)).astype(BF16)
+            near[q, side, 1] = to_side(
+                side, near_out.at[q, side, part], near_in.at[q, side, part],
+                near_send.at[q, side, 1], near_recv.at[q, side, 1],
+            )
 
     step = 64
-    for q in range(chunks):
-        for s in range(3):
-            x_copies[3 * q + s].wait_recv()
+
+    def finish(q):
+        for side in range(2):
+            for n in range(2):
+                near[q, side, n].wait_recv()
 
         @pl.loop(0, slots // step)
         def _(r):
             rows = pl.ds(pl.multiple_of(r * step, step), step)
             both = own[q, rows, :]
-            for s in range(3):
-                both = both + xrecv[q, s, rows, :].astype(F32)
+            for side in range(2):
+                both = both + near_in[q, side, rows, :].astype(F32)
             tiled = (step // 8, 8, LANES)
             real, imag = both[:, :LANES].reshape(tiled), both[:, LANES:].reshape(tiled)
             cut = limit[rows, :].reshape(tiled)
@@ -239,25 +312,31 @@
 
         zsend[q] = weave[...].reshape(zsend.shape[1:]).astype(BF16)
 
-        @pl.loop(0, nb - 1)
-        def _(i):
-            peer = plane_peer(i)
-            pltpu.make_async_remote_copy(
-                zsend.at[q, peer], out_ref.at[q, beam], z_send.at[q], z_recv.at[q],
-                device_id={"beam": peer}, device_id_type=MESH,
-            ).start()
-
+        start_plane_sends(lambda peer: zsend.at[q, peer], out_ref.at[q, beam], z_send.at[q], z_recv.at[q])
         pltpu.make_async_copy(zsend.at[q, beam], out_ref.at[q, beam], self_sem.at[q]).start()
+
+    form(0)
+    start_far(0)
+    start_near(0)
+    form(1)
+    for q in range(chunks):
+        relay(q)
+        if q + 1 < chunks:
+            start_far(q + 1)
+            start_near(q + 1)
+        if q + 2 < chunks:
+            form(q + 2)
+        finish(q)
 
     for q in range(chunks):
         arrived = out_ref.at[q, pl.ds(0, nb - 1)]
         pltpu.make_async_copy(arrived, arrived, z_recv.at[q]).wait()
         pltpu.make_async_copy(zsend.at[q, beam], out_ref.at[q, beam], self_sem.at[q]).wait()
 
-    pltpu.make_async_copy(everyone, everyone, ar_send).wait()
+    pltpu.make_async_copy(nearby, nearby, ar_send.at[0]).wait()
+    pltpu.make_async_copy(everyone, everyone, ar_send.at[1]).wait()
     send_echo.wait_send()
     send_perm.wait_send()
-    send_gain.wait_send()
     for copy in x_copies:
         copy.wait_send()
     for q in range(chunks):
@@ -295,18 +374,24 @@
             pltpu.VMEM((blocks, LANES, LANES), F32),
             pltpu.VMEM((2, 4, slots, 2 * chans), BF16),
             pltpu.VMEM((4, slots, 2 * chans), BF16),
-            pltpu.VMEM((nb, chans // LANES, LANES), F32),
+            pltpu.VMEM((9, chans // LANES, LANES), F32),
+            pltpu.VMEM((3, chans // LANES, LANES), F32),
+            pltpu.VMEM((24, chans // LANES, LANES), F32),
             pltpu.VMEM((2, chans // LANES, LANES), F32),
+            pltpu.VMEM((2, chans // LANES, LANES, LANES), F32),
             pltpu.VMEM((slots, LANES), F32),
             pltpu.VMEM((slots, LANES), F32),
             pltpu.VMEM((chunks, 2, 2 * chans, 2 * LANES), BF16),
-            pltpu.VMEM((chunks, 3, slots, 2 * LANES), BF16),
+            pltpu.VMEM((chunks, 2, slots // 2, 2 * LANES), BF16),
+            pltpu.VMEM((chunks, 2, slots // 2, 2 * LANES), BF16),
+            pltpu.VMEM((chunks, 2, slots, 2 * LANES), BF16),
+            pltpu.VMEM((chunks, 2, slots, 2 * LANES), BF16),
+            pltpu.VMEM((chunks, 2, slots // 2, 2 * LANES), F32),
             pltpu.VMEM((chunks, slots, 2 * LANES), F32),
-            pltpu.VMEM((chunks, 3, slots, 2 * LANES), BF16),
             pltpu.VMEM((2 * slots, LANES), F32),
             pltpu.VMEM((chunks, nb, rows, LANES), BF16),
-            dma((6,)), dma, dma, dma((3,)), dma((3,)),
-            dma((chunks, 3)), dma((chunks, 3)), dma((chunks,)), dma((chunks,)), dma((chunks,)),
+            dma((6,)), dma((2,)), dma((2,)), dma((2,)), dma((2,)),
+            dma((chunks, 2)), dma((chunks, 2)), dma((chunks, 2, 2)), dma((chunks, 2, 2)), dma((chunks,)), dma((chunks,)), dma((chunks,)),
         ],
         compiler_params=pltpu.CompilerParams(
             collective_id=0, has_side_effects=True, vmem_limit_bytes=40 << 20

time: 67.5 us -> 64 us (0.948)
  the two profiles are of different devices: /device:TPU:24 before, /device:TPU:2 now
where the time goes in v3:
time: 64 us; the launch traced here: 63.9 us
  Pallas kernels  63.8 us (100%)
    pallas_call x1, Pallas kernels, exchange(): pl.pallas_call(body, out_shape=jax.ShapeDtypeStruct((chunks, nb, rows, LA...  61.4 us
    pallas_call x1, Pallas kernels, doppler(): pl.pallas_call(dft_kernel, grid=(rows // 2,), out_shape=jax.ShapeDtypeStr...  2.43 us

profile of v3, /device:TPU:2, one launch (start us, length us, event | category | flops | bytes accessed | tf_op | source)
XLA Modules:
  0.0 63.9 jit_solution(3542845152563396702)
XLA Ops:
  0.0 0.0 copy-start.1
  0.0 0.0 copy-start
  0.0 61.4 %exchange.1.x_ref = bf16[4,64,8,128]{3,2,1,0:T(8,128)(2,1)S(1)} custom-call(bf16[2,256,512]{2,1,0:T(8,128)(2,1)} %refs_0_.1, bf16[2,2048,256]{2,1,0:T(8,128)(2,1)} %refs_1_.1, s32[16,128]{1,0:T(8,128)} %bitcast.3, s32[16,128]{1,0:T(8,128)} %bitcast.4, s32[16,128]{1,0:T(8,128)} %bitcast.5, bf16[2,8]{1,0:T(2,128)(2,1)} %refs_5_.1), custom_call_target="tpu_custom_call" | custom-call | tf_op jit(solution)/shard_map/exchange/pallas_call | solution.py:361
  61.4 0.0 copy-done.1
  61.4 0.0 copy-done
  61.4 2.4 %doppler.1 = f32[4,2,32,1024]{3,2,1,0:T(8,128)} custom-call(bf16[4,64,8,128]{3,2,1,0:T(8,128)(2,1)S(1)} %exchange.1.x_ref, bf16[512,512]{1,0:T(8,128)(2,1)S(1)} %copy-done, f32[8,256]{1,0:T(8,128)S(1)} %copy-done.1), custom_call_target="tpu_custom_call" | custom-call | tf_op jit(solution)/shard_map/doppler/pallas_call | solution.py:464
Async XLA Ops:
  0.0 61.4 %copy-start.1 = (f32[8,256]{1,0:T(8,128)S(1)}, f32[8,256]{1,0:T(8,128)}, u32[]{:S(2)}) copy-start(f32[8,256]{1,0:T(8,128)} %constant.5.clone.twist_ref) | copy-start | bytes 24580
  0.0 61.4 %copy-start = (bf16[512,512]{1,0:T(8,128)(2,1)S(1)}, bf16[512,512]{1,0:T(8,128)(2,1)}, u32[]{:S(2)}) copy-start(bf16[512,512]{1,0:T(8,128)(2,1)} %constant.4.clone.table_ref) | copy-start | bytes 1572868

commit v4 on v3

--- a/solution.py
+++ b/solution.py
@@ -21,7 +21,7 @@
     echo_hbm, steer_hbm, order_hbm, dwell_hbm, lens_hbm, code_hbm,
     out_ref,
     order_ref, dwell_ref, lens_ref, code_ref, coef,
-    echo, steer, cols, perm, perm_out, power, stage, gathered, gains, spread, limit, pulses, rhs, far_out, far_in, near_out, near_in, hold, own, weave, zsend,
+    echo, steer, cols, perm, perm_out, power, stage, gathered, gains, spread, limit, pulses, rhs, far_out, far_in, near_out, near_in, hold, own, weave, zsend, zrecv, wide,
     local_sem, ar_send, ar_recv, pair_send, pair_recv, far_send, far_recv, near_send, near_recv, z_send, z_recv, self_sem,
 ):
     nz = min(16, nb)
@@ -49,24 +49,25 @@
     def at(side, y, z):
         return {"tile": side, "beam": y * nz + z}
 
-    def start_plane_sends(source, target, sent, received):
-        def send(y, z):
-            peer = y * nz + z
+    def start_plane_sends(q, steps):
+        def send(k, z):
             pltpu.make_async_remote_copy(
-                source(peer), target, sent, received, device_id={"beam": peer}, device_id_type=MESH
+                zsend.at[q, k, z], zrecv.at[q, beam], z_send.at[q], z_recv.at[q],
+                device_id={"beam": ys[k] * nz + z}, device_id_type=MESH,
             ).start()
 
-        for y in ys:
-            send(y, zs(nz // 2))
+        for k in steps:
+            send(k, zs(nz // 2))
 
         @pl.loop(1, nz // 2)
         def _(m):
-            for z in (zs(nz // 2 + m - nz), zs(nz // 2 - m)):
-                for y in ys:
-                    send(y, z)
-
-        for y in ys[1:]:
-            send(y, my_z)
+            for z in (zs(m - nz // 2), zs(nz // 2 - m)):
+                for k in steps:
+                    send(k, z)
+
+        for k in steps:
+            if k > 0:
+                send(k, my_z)
 
     get_echo = pltpu.make_async_copy(echo_hbm, echo.at[core], local_sem.at[0])
     get_steer = pltpu.make_async_copy(steer_hbm, steer, local_sem.at[1])
@@ -87,18 +88,14 @@
 
     sides = [lax.rem(chip_x + d, 4) for d in (1, 3)]
     greeted = [at(tile, my_y, zs(d)) for d in (-4, -3, -2, -1, 1, 2, 3, 4)]
-    greeted += [at(tile, y, zs(d)) for y in ys[1:] for d in (0, 4, -4)]
-    greeted += [at(other, y, zs(d)) for y in ys for d in (0, 4, -4)]
-    greeted += [{"tile": 2 * side + core} for side in sides]
+    greeted += [at(tile, y, my_z) for y in ys[1:]]
+    greeted += [at(other, y, my_z) for y in ys]
+    across = lax.rem(chip_x + 2, 4)
+    greeted += [{"tile": 2 * side + core} for side in sides + [across]]
     for peer in greeted:
         pl.semaphore_signal(barrier, inc=1, device_id=peer, device_id_type=MESH)
 
-    small[0].wait()
-    order_cols = order_ref[...].astype(F32)
     lane = lax.broadcasted_iota(jnp.int32, (LANES, LANES), 1)
-    for b in range(blocks):
-        cols[b] = jnp.broadcast_to(order_cols[b : b + 1, :], (LANES, LANES)).T
-
     get_echo.wait()
     for v in range(nlane):
         total = jnp.zeros((LANES, LANES), F32)
@@ -119,8 +116,6 @@
         left = jnp.dot(hot, steer[0], preferred_element_type=F32)
         right = jnp.dot(hot, steer[1], preferred_element_type=F32)
         return left.astype(BF16), right.astype(BF16)
-
-    get_steer.wait()
 
     def permute(target, side, first, last):
         @pl.loop(first, last)
@@ -132,7 +127,12 @@
             target[dest, rows, :chans] = left
             target[dest, rows, chans:] = right
 
-    permute(perm_out, 1 - core, 0, 2 * half_blocks)
+    small[0].wait()
+    order_cols = order_ref[...].astype(F32)
+    for b in range(blocks):
+        cols[b] = jnp.broadcast_to(order_cols[b : b + 1, :], (LANES, LANES)).T
+    get_steer.wait()
+    permute(perm_out, 1 - core, 0, half_blocks)
     pl.semaphore_wait(barrier, len(greeted))
 
     for d in (-4, 4, -3, 3, -2, 2, -1, 1):
@@ -146,14 +146,12 @@
         device_id={"tile": other}, device_id_type=MESH,
     )
     send_echo.start()
-    permute(perm_out, 1 - core, 2 * half_blocks, 4 * half_blocks)
+    permute(perm_out, 1 - core, half_blocks, 4 * half_blocks)
     send_perm = pltpu.make_async_remote_copy(
         perm_out, perm.at[core], pair_send.at[1], pair_recv.at[1],
         device_id={"tile": other}, device_id_type=MESH,
     )
     send_perm.start()
-    permute(perm.at[core], core, 0, 2 * half_blocks)
-
     nearby = power.at[pl.ds(0, 8)]
     pltpu.make_async_copy(nearby, nearby, ar_recv.at[0]).wait()
     around = jnp.sum(power[...], axis=0)
@@ -170,7 +168,7 @@
                     stage.at[kind], gathered.at[(core * 3 + kind) * ny + my_y], ar_send.at[1], ar_recv.at[1],
                     device_id=at(side, y, zs(d)), device_id_type=MESH,
                 ).start()
-    permute(perm.at[core], core, 2 * half_blocks, 4 * half_blocks)
+    permute(perm.at[core], core, 0, 4 * half_blocks)
 
     for copy in small[1:]:
         copy.wait()
@@ -226,15 +224,14 @@
             perm[1, dest], rhs[q, 1], preferred_element_type=F32
         )
 
-    half = slots // 2
-    direct = [slice(half, slots), slice(0, half)]
-    summed = [slice(0, half), slice(half, slots)]
+    units = [(0, (k,)) for k in range(ny)] + [(q, tuple(range(ny))) for q in range(1, chunks)]
+    places = [lax.rem(y + ny - my_y, ny) for y in range(ny)]
+    block = (ny, 2, slots // (2 * ny), 2 * LANES)
     x_copies = []
 
-    def to_side(side, source, target, sent, received):
+    def to_chip(chip, source, target, sent, received):
         copy = pltpu.make_async_remote_copy(
-            source, target, sent, received,
-            device_id={"tile": 2 * sides[side] + core}, device_id_type=MESH,
+            source, target, sent, received, device_id={"tile": 2 * chip + core}, device_id_type=MESH
         )
         copy.start()
         x_copies.append(copy)
@@ -242,55 +239,69 @@
 
     far, near = {}, {}
 
-    def form(q):
-        scale(0, q)
-        scale(1, q)
-        product = partial_beams(q, lax.rem(chip_x + 2, 4))
+    def start_far(n):
+        q, steps = units[n]
+        span = pl.ds(steps[0], len(steps))
         for side in range(2):
-            far_out[q, side] = product[summed[side]].astype(BF16)
+            far[n, side] = to_chip(
+                across if n == 0 else sides[side], far_out.at[q, side, span], far_in.at[q, side, span],
+                far_send.at[n, side], far_recv.at[n, side],
+            )
+
+    def start_near(n, side, part, which):
+        q, steps = units[n]
+        span = pl.ds(steps[0], len(steps))
+        near[n, side, which] = to_chip(
+            sides[side], near_out.at[q, side, part, span], near_in.at[q, side, part, span],
+            near_send.at[n, side, which], near_recv.at[n, side, which],
+        )
+
+    def form_far(q):
+        product = partial_beams(q, across).reshape(block)
+        for y in range(ny):
+            for side in range(2):
+                far_out[q, side, places[y]] = product[y, side].astype(BF16)
+
+    def form_near(q, side):
+        product = partial_beams(q, sides[side]).reshape(block)
+        for y in range(ny):
+            near_out[q, side, 1 - side, places[y]] = product[y, 1 - side].astype(BF16)
+            hold[q, side, places[y]] = product[y, side]
+            if q == 0:
+                near_out[q, side, side, places[y]] = product[y, side].astype(BF16)
+
+    def form_own(q):
+        product = partial_beams(q, chip_x).reshape(block)
+        for y in range(ny):
+            own[q, places[y]] = product[y].reshape(slots // ny, 2 * LANES)
+
+    def relay(n):
+        q, steps = units[n]
         for side in range(2):
-            product = partial_beams(q, sides[side])
-            near_out[q, side, direct[side]] = product[direct[side]].astype(BF16)
-            hold[q, side] = product[summed[side]]
-        own[q] = partial_beams(q, chip_x)
-
-    def start_far(q):
+            far[n, side].wait_recv()
+            for k in steps:
+                near_out[q, side, side, k] = (hold[q, side, k] + far_in[q, side, k].astype(F32)).astype(BF16)
+            start_near(n, side, side, 1)
+
+    step = slots // ny
+
+    def finish(n):
+        q, steps = units[n]
         for side in range(2):
-            far[q, side] = to_side(
-                side, far_out.at[q, side], far_in.at[q, side], far_send.at[q, side], far_recv.at[q, side]
-            )
-
-    def start_near(q):
-        for side in range(2):
-            part = direct[side]
-            near[q, side, 0] = to_side(
-                side, near_out.at[q, side, part], near_in.at[q, side, part],
-                near_send.at[q, side, 0], near_recv.at[q, side, 0],
-            )
-
-    def relay(q):
-        for side in range(2):
-            far[q, side].wait_recv()
-            part = summed[side]
-            near_out[q, side, part] = (hold[q, side] + far_in[q, side].astype(F32)).astype(BF16)
-            near[q, side, 1] = to_side(
-                side, near_out.at[q, side, part], near_in.at[q, side, part],
-                near_send.at[q, side, 1], near_recv.at[q, side, 1],
-            )
-
-    step = 64
-
-    def finish(q):
-        for side in range(2):
-            for n in range(2):
-                near[q, side, n].wait_recv()
-
-        @pl.loop(0, slots // step)
-        def _(r):
-            rows = pl.ds(pl.multiple_of(r * step, step), step)
-            both = own[q, rows, :]
+            for which in range(2):
+                near[n, side, which].wait_recv()
+            if n == 0:
+                far[n, side].wait_recv()
+
+        def block_of(k, y):
+            rows = pl.ds(pl.multiple_of(y * step, step), step)
+            both = own[q, k]
             for side in range(2):
-                both = both + near_in[q, side, rows, :].astype(F32)
+                both = both + jnp.concatenate(
+                    [near_in[q, side, part, k].astype(F32) for part in range(2)], axis=0
+                )
+            if n == 0:
+                both = both + jnp.concatenate([far_in[q, part, k].astype(F32) for part in range(2)], axis=0)
             tiled = (step // 8, 8, LANES)
             real, imag = both[:, :LANES].reshape(tiled), both[:, LANES:].reshape(tiled)
             cut = limit[rows, :].reshape(tiled)
@@ -307,31 +318,70 @@
                 out_re = out_re + (code_re * shift_re + code_im * shift_im)
                 out_im = out_im + (code_re * shift_im - code_im * shift_re)
             kept = pulses[rows, :].reshape(tiled) > float(q * (LANES // G))
-            weave[pl.ds(r * (2 * step), step, stride=2), :] = jnp.where(kept, out_re, 0.0).reshape(step, LANES)
-            weave[pl.ds(r * (2 * step) + 1, step, stride=2), :] = jnp.where(kept, out_im, 0.0).reshape(step, LANES)
-
-        zsend[q] = weave[...].reshape(zsend.shape[1:]).astype(BF16)
-
-        start_plane_sends(lambda peer: zsend.at[q, peer], out_ref.at[q, beam], z_send.at[q], z_recv.at[q])
-        pltpu.make_async_copy(zsend.at[q, beam], out_ref.at[q, beam], self_sem.at[q]).start()
-
-    form(0)
-    start_far(0)
-    start_near(0)
-    form(1)
+            weave[k, pl.ds(0, step, stride=2), :] = jnp.where(kept, out_re, 0.0).reshape(step, LANES)
+            weave[k, pl.ds(1, step, stride=2), :] = jnp.where(kept, out_im, 0.0).reshape(step, LANES)
+            zsend[q, k] = weave[k].reshape(zsend.shape[2:]).astype(BF16)
+
+        if len(steps) == 1:
+            block_of(steps[0], ys[steps[0]])
+        else:
+
+            @pl.loop(0, ny)
+            def _(k):
+                block_of(k, lax.rem(my_y + k, ny))
+
+        start_plane_sends(q, steps)
+        if 0 in steps:
+            pltpu.make_async_copy(zsend.at[q, 0, my_z], zrecv.at[q, beam], self_sem.at[q]).start()
+
+    scale(0, 0)
+    scale(1, 0)
+    form_far(0)
+    for n in range(ny):
+        start_far(n)
+    for side in range(2):
+        form_near(0, side)
+        start_near(0, side, 1 - side, 0)
+        start_near(0, side, side, 1)
+    for side in range(2):
+        for n in range(1, ny):
+            start_near(n, side, 1 - side, 0)
+    def form_rest(q):
+        scale(0, q)
+        scale(1, q)
+        form_far(q)
+        form_near(q, 0)
+        form_near(q, 1)
+        form_own(q)
+
+    def start_rest(n):
+        start_far(n)
+        for side in range(2):
+            start_near(n, side, 1 - side, 0)
+
+    form_own(0)
+    form_rest(1)
+    form_rest(2)
+    form_rest(3)
+    for n in range(1, ny):
+        relay(n)
+    start_rest(ny)
+    for n in range(ny):
+        finish(n)
+    for n in range(ny, len(units)):
+        relay(n)
+        if n + 1 < len(units):
+            start_rest(n + 1)
+        finish(n)
+
     for q in range(chunks):
-        relay(q)
-        if q + 1 < chunks:
-            start_far(q + 1)
-            start_near(q + 1)
-        if q + 2 < chunks:
-            form(q + 2)
-        finish(q)
-
-    for q in range(chunks):
-        arrived = out_ref.at[q, pl.ds(0, nb - 1)]
+        arrived = zrecv.at[q, pl.ds(0, nb - 1)]
         pltpu.make_async_copy(arrived, arrived, z_recv.at[q]).wait()
-        pltpu.make_async_copy(zsend.at[q, beam], out_ref.at[q, beam], self_sem.at[q]).wait()
+        pltpu.make_async_copy(zsend.at[q, 0, my_z], zrecv.at[q, beam], self_sem.at[q]).wait()
+        wide[...] = zrecv[q].astype(F32).reshape(wide.shape)
+        for slot in range(4):
+            pair = [wide[pl.ds(2 * slot + c, nb, stride=8), :] for c in range(2)]
+            out_ref[slot, :, q * LANES : (q + 1) * LANES] = jnp.concatenate(pair, axis=0).T.astype(BF16)
 
     pltpu.make_async_copy(nearby, nearby, ar_send.at[0]).wait()
     pltpu.make_async_copy(everyone, everyone, ar_send.at[1]).wait()
@@ -340,7 +390,7 @@
     for copy in x_copies:
         copy.wait_send()
     for q in range(chunks):
-        sent = zsend.at[q, pl.ds(0, nb - 1)]
+        sent = zrecv.at[q, pl.ds(0, nb - 1)]
         pltpu.make_async_copy(sent, sent, z_send.at[q]).wait()
 
 
@@ -349,7 +399,7 @@
     total = steer.shape[1]
     slots = total // 8
     chunks = columns // LANES
-    rows = 2 * slots // nb
+    units = chunks + 3
     blocks = total // LANES
     vmem = pl.BlockSpec(memory_space=pltpu.VMEM)
     hbm = pl.BlockSpec(memory_space=pltpu.HBM)
@@ -360,7 +410,7 @@
 
     return pl.pallas_call(
         body,
-        out_shape=jax.ShapeDtypeStruct((chunks, nb, rows, LANES), BF16),
+        out_shape=jax.ShapeDtypeStruct((slots // nb, LANES, 2 * nb * chunks), BF16),
         in_specs=[hbm] * 6,
         out_specs=vmem,
         scratch_shapes=[
@@ -382,16 +432,18 @@
             pltpu.VMEM((slots, LANES), F32),
             pltpu.VMEM((slots, LANES), F32),
             pltpu.VMEM((chunks, 2, 2 * chans, 2 * LANES), BF16),
-            pltpu.VMEM((chunks, 2, slots // 2, 2 * LANES), BF16),
-            pltpu.VMEM((chunks, 2, slots // 2, 2 * LANES), BF16),
-            pltpu.VMEM((chunks, 2, slots, 2 * LANES), BF16),
-            pltpu.VMEM((chunks, 2, slots, 2 * LANES), BF16),
-            pltpu.VMEM((chunks, 2, slots // 2, 2 * LANES), F32),
-            pltpu.VMEM((chunks, slots, 2 * LANES), F32),
-            pltpu.VMEM((2 * slots, LANES), F32),
-            pltpu.VMEM((chunks, nb, rows, LANES), BF16),
+            pltpu.VMEM((chunks, 2, 4, slots // 8, 2 * LANES), BF16),
+            pltpu.VMEM((chunks, 2, 4, slots // 8, 2 * LANES), BF16),
+            pltpu.VMEM((chunks, 2, 2, 4, slots // 8, 2 * LANES), BF16),
+            pltpu.VMEM((chunks, 2, 2, 4, slots // 8, 2 * LANES), BF16),
+            pltpu.VMEM((chunks, 2, 4, slots // 8, 2 * LANES), F32),
+            pltpu.VMEM((chunks, 4, slots // 4, 2 * LANES), F32),
+            pltpu.VMEM((4, slots // 2, LANES), F32),
+            pltpu.VMEM((chunks, 4, nb // 4, 8, LANES), BF16),
+            pltpu.VMEM((chunks, nb, 8, LANES), BF16),
+            pltpu.VMEM((nb * 8, LANES), F32),
             dma((6,)), dma((2,)), dma((2,)), dma((2,)), dma((2,)),
-            dma((chunks, 2)), dma((chunks, 2)), dma((chunks, 2, 2)), dma((chunks, 2, 2)), dma((chunks,)), dma((chunks,)), dma((chunks,)),
+            dma((units, 2)), dma((units, 2)), dma((units, 2, 2)), dma((units, 2, 2)), dma((chunks,)), dma((chunks,)), dma((chunks,)),
         ],
         compiler_params=pltpu.CompilerParams(
             collective_id=0, has_side_effects=True, vmem_limit_bytes=40 << 20
@@ -412,28 +464,20 @@
 def dft_tables(nb, chunks, pulses_all):
     length = nb * chunks
     radix = pulses_all // length
-    index = (np.arange(nb)[None, :] * chunks + np.arange(chunks)[:, None]).reshape(-1)
-    angle = -2.0 * np.pi * ((index[:, None] * np.arange(length)[None, :]) % length) / length
+    index = np.arange(nb)[None, :] * chunks + np.arange(chunks)[:, None]
+    angle = -2.0 * np.pi * ((index[:, :, None] * np.arange(length)) % length) / length
     real, imag = np.cos(angle), np.sin(angle)
-    table = np.block([[real, imag], [-imag, real]])
+    table = np.concatenate(
+        [np.concatenate([real, imag], axis=2), np.concatenate([-imag, real], axis=2)], axis=1
+    ).reshape(2 * length, 2 * length)
     turn = -2.0 * np.pi * np.arange(radix)[:, None] * np.arange(length)[None, :] / pulses_all
     twist = np.concatenate([np.cos(turn), np.sin(turn)], axis=0) / math.sqrt(pulses_all)
     return jnp.asarray(table, BF16), jnp.asarray(twist, F32)
 
 
-def dft_kernel(x_ref, table_ref, twist_ref, out_ref, wide):
-    chunks, nb, rows, _ = x_ref.shape
-    length = chunks * nb
-    slot = pl.program_id(0)
-
-    @pl.when(slot == 0)
-    def _():
-        wide[...] = x_ref[...].astype(F32).reshape(wide.shape)
-
-    real = wide[pl.ds(2 * slot, length, stride=rows), :].T.astype(BF16)
-    imag = wide[pl.ds(2 * slot + 1, length, stride=rows), :].T.astype(BF16)
-    left = jnp.concatenate([real, imag], axis=1)
-    found = jnp.dot(left, table_ref[...], preferred_element_type=F32)
+def dft_kernel(x_ref, table_ref, twist_ref, out_ref):
+    length = x_ref.shape[2] // 2
+    found = jnp.dot(x_ref[pl.program_id(0)], table_ref[...], preferred_element_type=F32)
     re, im = [], []
     for p in range(4):
         fr = found[p * G : (p + 1) * G, :length]
@@ -457,17 +501,16 @@
         out_ref[0, 1, :, k * length : (k + 1) * length] = b
 
 
-def doppler(x, pulses_all):
-    chunks, nb, rows, _ = x.shape
-    table, twist = dft_tables(nb, chunks, pulses_all)
+def doppler(x, nb, pulses_all):
+    slots, _, width = x.shape
+    table, twist = dft_tables(nb, width // (2 * nb), pulses_all)
     vmem = pl.BlockSpec(memory_space=pltpu.VMEM)
     return pl.pallas_call(
         dft_kernel,
-        grid=(rows // 2,),
-        out_shape=jax.ShapeDtypeStruct((rows // 2, 2, G, pulses_all), F32),
+        grid=(slots,),
+        out_shape=jax.ShapeDtypeStruct((slots, 2, G, pulses_all), F32),
         in_specs=[vmem, vmem, vmem],
         out_specs=pl.BlockSpec((1, 2, G, pulses_all), lambda n: (n, 0, 0, 0)),
-        scratch_shapes=[pltpu.VMEM((chunks * nb * rows, LANES), F32)],
         compiler_params=pltpu.CompilerParams(vmem_limit_bytes=8 << 20),
         name="doppler",
     )(x, table, twist)
@@ -478,7 +521,7 @@
 
     def on_device(echoes, steer, code, beam_order, dwell, code_len):
         arrived = exchange(nb, echoes, steer, code, beam_order, dwell, code_len)
-        return doppler(arrived, nb * echoes.shape[2] // G)
+        return doppler(arrived, nb, nb * echoes.shape[2] // G)
 
     placed = (P(None, "tile", "beam"), P(None, None, "tile"), P(), P(), P(), P())
     return jax.shard_map(

time: 64 us -> 61.4 us (0.959)
  the two profiles are of different devices: /device:TPU:2 before, /device:TPU:24 now
where the time goes in v4:
time: 61.4 us; the launch traced here: 60.8 us
  Pallas kernels  60.8 us (99%)
    pallas_call x1, Pallas kernels, exchange(): pl.pallas_call(body, out_shape=jax.ShapeDtypeStruct((slots // nb, LANES,...  58.6 us
    pallas_call x1, Pallas kernels, doppler(): pl.pallas_call(dft_kernel, grid=(slots,), out_shape=jax.ShapeDtypeStruct(...  2.2 us

profile of v4, /device:TPU:24, one launch (start us, length us, event | category | flops | bytes accessed | tf_op | source)
XLA Modules:
  0.0 60.8 jit_solution(3814358634127229555)
XLA Ops:
  0.0 0.0 copy-start.1
  0.0 0.0 copy-start
  0.0 58.6 %exchange.1.x_ref = bf16[4,128,512]{2,1,0:T(8,128)(2,1)S(1)} custom-call(bf16[2,256,512]{2,1,0:T(8,128)(2,1)} %refs_0_.1, bf16[2,2048,256]{2,1,0:T(8,128)(2,1)} %refs_1_.1, s32[16,128]{1,0:T(8,128)} %bitcast.3, s32[16,128]{1,0:T(8,128)} %bitcast.4, s32[16,128]{1,0:T(8,128)} %bitcast.5, bf16[2,8]{1,0:T(2,128)(2,1)} %refs_5_.1), custom_call_target="tpu_custom_call" | custom-call | tf_op jit(solution)/shard_map/exchange/pallas_call | solution.py:411
  58.6 0.0 copy-done.1
  58.6 0.0 copy-done
  58.6 2.2 %doppler.1 = f32[4,2,32,1024]{3,2,1,0:T(8,128)} custom-call(bf16[4,128,512]{2,1,0:T(8,128)(2,1)S(1)} %exchange.1.x_ref, bf16[512,512]{1,0:T(8,128)(2,1)S(1)} %copy-done, f32[8,256]{1,0:T(8,128)S(1)} %copy-done.1), custom_call_target="tpu_custom_call" | custom-call | tf_op jit(solution)/shard_map/doppler/pallas_call | solution.py:508
Async XLA Ops:
  0.0 58.6 %copy-start.1 = (f32[8,256]{1,0:T(8,128)S(1)}, f32[8,256]{1,0:T(8,128)}, u32[]{:S(2)}) copy-start(f32[8,256]{1,0:T(8,128)} %constant.5.clone.twist_ref) | copy-start | bytes 24580
  0.0 58.6 %copy-start = (bf16[512,512]{1,0:T(8,128)(2,1)S(1)}, bf16[512,512]{1,0:T(8,128)(2,1)}, u32[]{:S(2)}) copy-start(bf16[512,512]{1,0:T(8,128)(2,1)} %constant.4.clone.table_ref) | copy-start | bytes 1572868

commit v5 on v4

--- a/solution.py
+++ b/solution.py
@@ -55,6 +55,19 @@
                 zsend.at[q, k, z], zrecv.at[q, beam], z_send.at[q], z_recv.at[q],
                 device_id={"beam": ys[k] * nz + z}, device_id_type=MESH,
             ).start()
+
+        if q == chunks - 1:
+
+            @pl.loop(0, nz)
+            def _(z):
+                for k in steps[1:]:
+                    send(k, z)
+
+                @pl.when(z != my_z)
+                def _():
+                    send(0, z)
+
+            return
 
         for k in steps:
             send(k, zs(nz // 2))
@@ -475,9 +488,9 @@
     return jnp.asarray(table, BF16), jnp.asarray(twist, F32)
 
 
-def dft_kernel(x_ref, table_ref, twist_ref, out_ref):
-    length = x_ref.shape[2] // 2
-    found = jnp.dot(x_ref[pl.program_id(0)], table_ref[...], preferred_element_type=F32)
+def dft_slot(x_ref, table_ref, twist_ref, out_ref):
+    length = x_ref.shape[1] // 2
+    found = jnp.dot(x_ref[...], table_ref[...], preferred_element_type=F32)
     re, im = [], []
     for p in range(4):
         fr = found[p * G : (p + 1) * G, :length]
@@ -497,8 +510,13 @@
         (odd_re - turn_im, odd_im + turn_re),
     ]
     for k, (a, b) in enumerate(parts):
-        out_ref[0, 0, :, k * length : (k + 1) * length] = a
-        out_ref[0, 1, :, k * length : (k + 1) * length] = b
+        out_ref[0, :, k * length : (k + 1) * length] = a
+        out_ref[1, :, k * length : (k + 1) * length] = b
+
+
+def dft_kernel(x_ref, table_ref, twist_ref, out_ref):
+    for n in range(out_ref.shape[0]):
+        dft_slot(x_ref.at[pl.program_id(0) * out_ref.shape[0] + n], table_ref, twist_ref, out_ref.at[n])
 
 
 def doppler(x, nb, pulses_all):
@@ -507,10 +525,10 @@
     vmem = pl.BlockSpec(memory_space=pltpu.VMEM)
     return pl.pallas_call(
         dft_kernel,
-        grid=(slots,),
+        grid=(slots // 2,),
         out_shape=jax.ShapeDtypeStruct((slots, 2, G, pulses_all), F32),
         in_specs=[vmem, vmem, vmem],
-        out_specs=pl.BlockSpec((1, 2, G, pulses_all), lambda n: (n, 0, 0, 0)),
+        out_specs=pl.BlockSpec((2, 2, G, pulses_all), lambda n: (n, 0, 0, 0)),
         compiler_params=pltpu.CompilerParams(vmem_limit_bytes=8 << 20),
         name="doppler",
     )(x, table, twist)

time: 61.4 us -> 59.7 us (0.972)
  Pallas kernels: 60.8 us -> 59 us
    pallas_call x1, Pallas kernels: 58.6 us -> 57.5 us  [exchange(): pl.pallas_call(body, out_shape=jax.ShapeDtypeStruct((slots // nb, LANES,...]
    pallas_call x1, Pallas kernels: 2.2 us -> 1.49 us  [doppler(): pl.pallas_call(dft_kernel, grid=(slots // 2,), out_shape=jax.ShapeDtypeSt...]
where the time goes in v5:
time: 59.7 us; the launch traced here: 59 us
  Pallas kernels  59 us (99%)
    pallas_call x1, Pallas kernels, exchange(): pl.pallas_call(body, out_shape=jax.ShapeDtypeStruct((slots // nb, LANES,...  57.5 us
    pallas_call x1, Pallas kernels, doppler(): pl.pallas_call(dft_kernel, grid=(slots // 2,), out_shape=jax.ShapeDtypeSt...  1.49 us

profile of v5, /device:TPU:24, one launch (start us, length us, event | category | flops | bytes accessed | tf_op | source)
XLA Modules:
  0.0 59.0 jit_solution(8091907797022900226)
XLA Ops:
  0.0 0.0 copy-start.1
  0.0 0.0 copy-start
  0.0 57.5 %exchange.1.x_ref = bf16[4,128,512]{2,1,0:T(8,128)(2,1)S(1)} custom-call(bf16[2,256,512]{2,1,0:T(8,128)(2,1)} %refs_0_.1, bf16[2,2048,256]{2,1,0:T(8,128)(2,1)} %refs_1_.1, s32[16,128]{1,0:T(8,128)} %bitcast.3, s32[16,128]{1,0:T(8,128)} %bitcast.4, s32[16,128]{1,0:T(8,128)} %bitcast.5, bf16[2,8]{1,0:T(2,128)(2,1)} %refs_5_.1), custom_call_target="tpu_custom_call" | custom-call | tf_op jit(solution)/shard_map/exchange/pallas_call | solution.py:424
  57.5 0.0 copy-done.1
  57.5 0.0 copy-done
  57.5 1.5 %doppler.1 = f32[4,2,32,1024]{3,2,1,0:T(8,128)} custom-call(bf16[4,128,512]{2,1,0:T(8,128)(2,1)S(1)} %exchange.1.x_ref, bf16[512,512]{1,0:T(8,128)(2,1)S(1)} %copy-done, f32[8,256]{1,0:T(8,128)S(1)} %copy-done.1), custom_call_target="tpu_custom_call" | custom-call | tf_op jit(solution)/shard_map/doppler/pallas_call | solution.py:526
Async XLA Ops:
  0.0 57.5 %copy-start.1 = (f32[8,256]{1,0:T(8,128)S(1)}, f32[8,256]{1,0:T(8,128)}, u32[]{:S(2)}) copy-start(f32[8,256]{1,0:T(8,128)} %constant.5.clone.twist_ref) | copy-start | bytes 24580
  0.0 57.5 %copy-start = (bf16[512,512]{1,0:T(8,128)(2,1)S(1)}, bf16[512,512]{1,0:T(8,128)(2,1)}, u32[]{:S(2)}) copy-start(bf16[512,512]{1,0:T(8,128)(2,1)} %constant.4.clone.table_ref) | copy-start | bytes 1572868
